TPU v7x, 128 devices: a whole 4x4x4 slice. The times are simulated.
128 devices in a mesh: rows: 8 (over z, core), cols: 16 (over x, y).
Axes of the slice: x: 4, y: 4, z: 4, core: 2. Of those that a mesh axis runs over, the one named last changes fastest.
Arguments:
- density: bfloat16 [6144, 6144], P('rows', 'cols')
- points: float32 [6144, 3, 256], P(('rows', 'cols')), may hold values from -1 to 1
- grid_weights: float32 [6144, 256], P(('rows', 'cols')), may hold values from 0.002 to 0.02
- centres: float32 [3, 6144], replicated, may hold values from -1 to 1
- exponents: float32 [6144], replicated, may hold values from 3 to 12
- sig_blocks: int32 [6144, 4], P(('rows', 'cols')), may hold values from 0 to 47, as said below
- live_count: int32 [128], P(('rows', 'cols')), may hold values from 1 to 48, as said below
Outputs:
- xc_diag: float32 [6144, 768], P('rows', 'cols')
- batch_energy: float32 [6144], P(('rows', 'cols'))
- exc_total: float32 [], replicated
Inputs may be any that keep to these rules, and one draw needn't show every extreme that they name: `sig_blocks`: each row holds 4 different blocks in rising order, all among the 48 // 8 blocks of the batch's row group. `live_count`: some device has all 48 slots in use.
All inputs are finite; a program needn't handle non-finite values.
Results may differ from a plain program's by a relative error of at most 0.0005.
Values may be sent and summed in bfloat16 or wider, within the bound.
No kernel may reach another device: no remote copies, remote signals or barrier semaphores. Data moves between devices by JAX's collectives and lax.ppermute only.
A program may use at most 64 MiB of HBM per device.

v0:
```python
import jax
import jax.numpy as jnp
from jax import lax
from jax.experimental import pallas as pl
from jax.experimental.pallas import tpu as pltpu
from jax.sharding import Mesh
from jax.sharding import PartitionSpec as P

BLOCK = 128
NSIG = 4
PTS = 256
SLOTS = 48
SPAN = 6
OWN = SPAN * BLOCK
NCOLS = 16
PER = SLOTS // NCOLS
STRIP = OWN // NCOLS
COLS = ("cols_0", "cols_1")
ROWS = ("rows_0", "rows_1")
ROWS_COLS = ("rows_0", "rows_1", "cols_0", "cols_1")

slater = 0.7386

VMEM = pl.BlockSpec(memory_space=pltpu.VMEM)
SMEM = pl.BlockSpec(memory_space=pltpu.SMEM)
ANY = pl.BlockSpec(memory_space=pltpu.HBM)
RING = 16
UNROLL = 4
LIMIT = 50
TOP = 32766.0
EXTRA = 16


def exchange(blocks):
    return lax.all_to_all(blocks, COLS, split_axis=0, concat_axis=0, tiled=True)


def column():
    return 4 * lax.axis_index("cols_0") + lax.axis_index("cols_1")


def pack_kernel(live_ref, dens_ref, pts_ref, w_ref, sig_ref, out_ref, pts_s, w_s, sig_s, tile_s, sem):
    strips = [
        pltpu.make_async_copy(
            dens_ref.at[d * STRIP : (d + 1) * STRIP], out_ref.at[d, :STRIP], sem.at[3 + d]
        )
        for d in range(NCOLS)
    ]
    inputs = [
        pltpu.make_async_copy(src, dst, sem.at[q])
        for q, (src, dst) in enumerate(((pts_ref, pts_s), (w_ref, w_s), (sig_ref, sig_s)))
    ]
    for copy in inputs + strips:
        copy.start()
    for copy in inputs:
        copy.wait()
    me = column()
    group = 2 * lax.axis_index("rows_0") + lax.axis_index("rows_1")
    local = (sig_s[...] - group * SPAN).astype(jnp.float32)
    slots = lax.broadcasted_iota(jnp.int32, (NSIG, SLOTS), 1)
    live = (slots < live_ref[0]).astype(jnp.float32)
    tags = jnp.concatenate([local, live], axis=0)

    def one(s, _):
        d = lax.rem(s + me, NCOLS)
        for k in range(PER):
            for c in range(4):
                src = w_s if c == 3 else pts_s.at[c]
                row = src[pl.ds(s + NCOLS * k, 1), :]
                for h in range(2):
                    tile_s[d, pl.ds(8 * k + 2 * c + h, 1), :] = row[:, h * 128 : (h + 1) * 128]
        tile_s[d, pl.ds(8 * PER, 8), :SLOTS] = tags
        return 0

    tile_s[:, 8 * PER :, :] = jnp.zeros((NCOLS, 8, 128), jnp.float32)
    lax.fori_loop(0, NCOLS, one, 0)
    for d in range(NCOLS):
        rest = tile_s[d]
        for q in range(3):
            part = rest.astype(jnp.bfloat16)
            rest = rest - part.astype(jnp.float32)
            out_ref[d, STRIP:, q * 128 : (q + 1) * 128] = part
    for copy in strips:
        copy.wait()


def phi_kernel(meta_ref, recv_ref, basis_ref, phi_ref, list_ref, tile_ref, ring_s, sem):
    me = column()
    for i in range(NCOLS):
        hi, mid, lo = (
            recv_ref[i, STRIP:, q * 128 : (q + 1) * 128].astype(jnp.float32) for q in range(3)
        )
        tile_ref[i] = (lo + mid) + hi

    def scan(i, n):
        s = lax.rem(me - i + NCOLS, NCOLS)
        for k in range(PER):
            code = meta_ref[i, s + NCOLS * k]
            list_ref[n] = (i * 4 + k) * 4096 + code
            n = n + (code >= 0).astype(jnp.int32)
        return n

    total = lax.fori_loop(0, NCOLS, scan, 0)
    list_ref[63] = total

    def save(n):
        slot = lax.rem(n, RING)
        return pltpu.make_async_copy(ring_s.at[slot], phi_ref.at[n], sem.at[slot])

    def one(n, _):
        @pl.when(n >= RING)
        def _():
            save(n - RING).wait()

        spot = lax.rem(n, RING)
        v = list_ref[n]
        slot = v // 4096
        code = v % 4096
        i = slot // 4
        k = slot % 4
        tile = tile_ref[i, pl.ds(pl.multiple_of(8 * k, 8), 8), :]
        for t in range(NSIG):
            l = (code >> (3 * t)) & 7
            rows = pl.ds(pl.multiple_of(l * BLOCK, BLOCK), BLOCK)
            cx, cy, cz, neg = (basis_ref[q, rows, :] for q in range(4))
            for h in range(2):
                gx = tile[h : h + 1] - cx
                gy = tile[2 + h : 3 + h] - cy
                gz = tile[4 + h : 5 + h] - cz
                dist = gx * gx + gy * gy + gz * gz
                ring_s[spot, t * BLOCK : (t + 1) * BLOCK, h * 128 : (h + 1) * 128] = jnp.exp(
                    neg * dist
                ).astype(jnp.bfloat16)
        save(n).start()
        return 0

    lax.fori_loop(0, total, one, 0)

    def drain(n, _):
        save(n).wait()
        return 0

    lax.fori_loop(jnp.maximum(total - RING, 0), total, drain, 0)


def xc_kernel(
    list_ref, dens_ref, phi_ref, tile_ref, out_ref, total_ref,
    dens_s, acc_s, scaled_s, image_s, factor_s, term_s, ring_s, sem,
):
    total = list_ref[63]

    def load(n):
        slot = lax.rem(n, RING)
        return pltpu.make_async_copy(phi_ref.at[n], ring_s.at[slot], sem.at[slot])

    for u in range(UNROLL):

        @pl.when(u < total)
        def _():
            load(u).start()

    for a in range(SPAN):
        for b in range(SPAN):
            dens_s[a * SPAN + b] = dens_ref[
                a * BLOCK : (a + 1) * BLOCK, b * BLOCK : (b + 1) * BLOCK
            ]
    acc_s[...] = jnp.zeros_like(acc_s)
    scaled_s[...] = jnp.zeros_like(scaled_s)
    image_s[...] = jnp.zeros_like(image_s)
    factor_s[...] = jnp.zeros_like(factor_s)
    term_s[...] = jnp.zeros_like(term_s)

    def locals_of(n):
        code = list_ref[n] % 4096
        return [(code >> (3 * t)) & 7 for t in range(NSIG)]

    def add_delta(n):
        loc = locals_of(n)
        slot = lax.rem(n, RING)
        for h in range(2):
            delta = lax.dot_general(
                scaled_s[...],
                ring_s[slot, h * 2 * BLOCK : (h + 1) * 2 * BLOCK, :],
                (((1,), (1,)), ((), ())),
                preferred_element_type=jnp.float32,
            )
            for a in range(NSIG):
                rows = pl.ds(pl.multiple_of(loc[a] * BLOCK, BLOCK), BLOCK)
                for b in range(2):
                    acc_s[loc[2 * h + b], rows, :] += delta[
                        a * BLOCK : (a + 1) * BLOCK, b * BLOCK : (b + 1) * BLOCK
                    ]

    def scale(n, live):
        factor = jnp.where(live, factor_s[...], 0.0)
        for t in range(NSIG):
            rows = slice(t * BLOCK, (t + 1) * BLOCK)
            phi = ring_s[lax.rem(n, RING), rows, :].astype(jnp.float32)
            scaled_s[rows, :] = (phi * factor).astype(jnp.bfloat16)

    def potential(n):
        slot = list_ref[n] // 4096
        i = slot // 4
        k = slot % 4
        phi = ring_s[lax.rem(n, RING)].astype(jnp.float32)
        rho = jnp.maximum(jnp.sum(phi * image_s[...], axis=0, keepdims=True), 0.0)
        root = jnp.exp2(jnp.log2(rho) * (1.0 / 3.0))
        w8 = tile_ref[i, pl.ds(pl.multiple_of(8 * k, 8), 8), :]
        weight = jnp.concatenate([w8[6:7], w8[7:8]], axis=1)
        term_s[pl.ds(slot, 1), :] = weight * (-slater) * rho * root
        factor_s[...] = weight * (-4.0 / 3.0 * slater) * root

    def image(n):
        loc = locals_of(n)
        p_ss = jnp.concatenate(
            [
                jnp.concatenate([dens_s[loc[a] * SPAN + loc[b]] for b in range(NSIG)], axis=1)
                for a in range(NSIG)
            ],
            axis=0,
        )
        image_s[...] = jnp.dot(p_ss, ring_s[lax.rem(n, RING)], preferred_element_type=jnp.float32)

    def one(m, _):
        first = m * UNROLL
        for u in range(UNROLL):

            @pl.when(first + UNROLL + u < total)
            def _():
                load(first + UNROLL + u).start()

        for u in range(UNROLL):

            @pl.when(first + u < total)
            def _():
                load(first + u).wait()

        for u in range(UNROLL):
            n = first + u
            add_delta(jnp.clip(n - 3, 0, last))
            scale(jnp.clip(n - 2, 0, last), n < total + 2)
            potential(jnp.clip(n - 1, 0, last))
            image(jnp.minimum(n, last))
        return 0

    last = total - 1

    @pl.when(total > 0)
    def _():
        lax.fori_loop(0, (total + 3 + UNROLL - 1) // UNROLL, one, 0)

    me = column()
    terms = jnp.broadcast_to(jnp.sum(term_s[...], axis=1, keepdims=True), (NCOLS * 4, 128))
    total_ref[...] = jnp.broadcast_to(jnp.sum(terms, axis=0, keepdims=True), total_ref.shape)
    peak = jnp.max(jnp.abs(terms), axis=0, keepdims=True)
    term_code = quarter_octaves(peak)
    terms = terms * (TOP * jnp.exp2(-0.25 * term_code))
    row = lax.broadcasted_iota(jnp.int32, (STRIP, 128), 0)
    lane = lax.broadcasted_iota(jnp.int32, (STRIP, 128), 1)
    line = lax.broadcasted_iota(jnp.int32, (EXTRA, 128), 0)
    slot = lane[:1]
    for j in range(NCOLS):
        rows = slice(j * STRIP, (j + 1) * STRIP)
        peak = jnp.abs(acc_s[0, rows, :])
        for b in range(1, SPAN):
            peak = jnp.maximum(peak, jnp.abs(acc_s[b, rows, :]))
        code = quarter_octaves(jnp.max(peak, axis=1, keepdims=True))
        scale = TOP * jnp.exp2(-0.25 * code)
        for b in range(SPAN):
            out_ref[j, b * STRIP : (b + 1) * STRIP, :] = to_short(acc_s[b, rows, :] * scale)
        s = lax.rem(me - j + NCOLS, NCOLS)
        energy = jnp.zeros((1, 128), jnp.float32)
        for k in range(PER):
            here = terms[4 * j + k : 4 * j + k + 1]
            energy = energy + jnp.where(slot == s + NCOLS * k, here, 0.0)
        high = jnp.round(energy)
        low = (energy - high) * (2.0 * TOP)
        codes = jnp.sum(jnp.where(row == lane, code, 0.0), axis=0, keepdims=True)
        extra = jnp.where(line == 0, high, jnp.where(line == 1, low, jnp.where(line == 2, codes, term_code)))
        out_ref[j, SPAN * STRIP :, :] = to_short(extra)


def quarter_octaves(peak):
    return jnp.clip(jnp.ceil(4.0 * jnp.log2(peak)), -480.0, 500.0)


def to_short(x):
    return jnp.round(x).astype(jnp.int32).astype(jnp.int16)


def merge_kernel(recv_ref, xc_ref, energy_ref):
    row = lax.broadcasted_iota(jnp.int32, (STRIP, 128), 0)
    lane = lax.broadcasted_iota(jnp.int32, (STRIP, 128), 1)
    energy = jnp.zeros((1, 128), jnp.float32)
    total = [jnp.zeros((STRIP, 128), jnp.float32) for _ in range(SPAN)]
    for j in range(NCOLS):
        extra = recv_ref[j, SPAN * STRIP :, :].astype(jnp.int32).astype(jnp.float32)
        unit = (1.0 / TOP) * jnp.exp2(0.25 * extra[2:4])
        scale = jnp.sum(jnp.where(row == lane, unit[:1], 0.0), axis=1, keepdims=True)
        for b in range(SPAN):
            part = recv_ref[j, b * STRIP : (b + 1) * STRIP, :].astype(jnp.int32)
            total[b] = total[b] + part.astype(jnp.float32) * scale
        energy = energy + (extra[:1] + extra[1:2] * (0.5 / TOP)) * unit[1:2]
    for b in range(SPAN):
        xc_ref[:, b * BLOCK : (b + 1) * BLOCK] = total[b]
    energy_ref[...] = energy[:, :SLOTS]


def over_all(value):
    left, far, right = (
        lax.ppermute(value, "cols_0", [(a, (a + hop) % 4) for a in range(4)])
        for hop in (1, 2, 3)
    )
    value = (value + far) + (left + right)
    for axis, other in (("rows_1", 1), ("rows_0", 1), ("rows_0", 3), ("cols_1", 1), ("cols_1", 3)):
        moved = lax.ppermute(value, axis, [(a, a ^ other) for a in range(lax.axis_size(axis))])
        value = value + moved
    return value


def shards(density, points, grid_weights, centres, exponents, sig_blocks, live_count):
    group = lax.axis_index(ROWS)

    packed = pl.pallas_call(
        pack_kernel,
        out_shape=jax.ShapeDtypeStruct((NCOLS, STRIP + 32, 384), jnp.bfloat16),
        in_specs=[SMEM, ANY, ANY, ANY, ANY],
        out_specs=VMEM,
        scratch_shapes=[
            pltpu.VMEM((3, SLOTS, PTS), jnp.float32),
            pltpu.VMEM((SLOTS, PTS), jnp.float32),
            pltpu.VMEM((NSIG, SLOTS), jnp.int32),
            pltpu.VMEM((NCOLS, 32, 128), jnp.float32),
            pltpu.SemaphoreType.DMA((3 + NCOLS,)),
        ],
        name="pack",
    )(live_count, density, points.transpose(1, 0, 2), grid_weights, sig_blocks.T)
    recv = exchange(packed)

    pair = lax.dynamic_slice(recv, (group * 2, 0, 0), (2, STRIP, 384))
    strip = jnp.concatenate([pair[0], pair[1]], axis=1)
    dens = exchange(jnp.broadcast_to(strip[None], (NCOLS, STRIP, OWN))).reshape(OWN, OWN)

    tags = recv[:, STRIP + 24 : STRIP + 29, :SLOTS].astype(jnp.int32)
    meta = tags[:, 0] + 8 * tags[:, 1] + 64 * tags[:, 2] + 512 * tags[:, 3]
    meta = jnp.where(tags[:, 4] > 0, meta, -1)

    own = jnp.concatenate(
        [
            lax.dynamic_slice_in_dim(centres, group * OWN, OWN, 1),
            -lax.dynamic_slice_in_dim(exponents, group * OWN, OWN, 0)[None],
        ],
        axis=0,
    )
    basis = jnp.broadcast_to(own[:, :, None], (4, OWN, 128))
    phi, batches, tiles = pl.pallas_call(
        phi_kernel,
        out_shape=(
            jax.ShapeDtypeStruct((SLOTS, NSIG * BLOCK, PTS), jnp.bfloat16),
            jax.ShapeDtypeStruct((64,), jnp.int32),
            jax.ShapeDtypeStruct((NCOLS, 32, 128), jnp.float32),
        ),
        in_specs=[SMEM, VMEM, VMEM],
        out_specs=(ANY, SMEM, VMEM),
        scratch_shapes=[
            pltpu.VMEM((RING, NSIG * BLOCK, PTS), jnp.bfloat16),
            pltpu.SemaphoreType.DMA((RING,)),
        ],
        compiler_params=pltpu.CompilerParams(vmem_limit_bytes=LIMIT << 20),
        cost_estimate=pl.CostEstimate(
            flops=10 * 32 * 512 * 256, transcendentals=32 * 512 * 256, bytes_accessed=16 << 20
        ),
        name="phi",
    )(meta, recv, basis)

    contrib, total = pl.pallas_call(
        xc_kernel,
        out_shape=(
            jax.ShapeDtypeStruct((NCOLS, SPAN * STRIP + EXTRA, BLOCK), jnp.int16),
            jax.ShapeDtypeStruct((8, 128), jnp.float32),
        ),
        in_specs=[SMEM, VMEM, ANY, VMEM],
        out_specs=(VMEM, VMEM),
        scratch_shapes=[
            pltpu.VMEM((SPAN * SPAN, BLOCK, BLOCK), jnp.bfloat16),
            pltpu.VMEM((SPAN, OWN, BLOCK), jnp.float32),
            pltpu.VMEM((NSIG * BLOCK, PTS), jnp.bfloat16),
            pltpu.VMEM((NSIG * BLOCK, PTS), jnp.float32),
            pltpu.VMEM((1, PTS), jnp.float32),
            pltpu.VMEM((NCOLS * 4, PTS), jnp.float32),
            pltpu.VMEM((RING, NSIG * BLOCK, PTS), jnp.bfloat16),
            pltpu.SemaphoreType.DMA((RING,)),
        ],
        compiler_params=pltpu.CompilerParams(vmem_limit_bytes=LIMIT << 20),
        cost_estimate=pl.CostEstimate(
            flops=32 * 4 * 512 * 512 * 256, transcendentals=0, bytes_accessed=16 << 20
        ),
        name="xc",
    )(batches, dens, phi, tiles)

    parts = exchange(contrib)
    exc_total = over_all(total)[0, 0]
    merge = pl.pallas_call(
        merge_kernel,
        out_shape=(
            jax.ShapeDtypeStruct((STRIP, OWN), jnp.float32),
            jax.ShapeDtypeStruct((1, SLOTS), jnp.float32),
        ),
        in_specs=[VMEM],
        out_specs=(VMEM, VMEM),
        compiler_params=pltpu.CompilerParams(vmem_limit_bytes=16 << 20),
        name="merge",
    )
    xc_rows, energy = merge(parts)
    return (xc_rows.T, energy.reshape(SLOTS), exc_total)


def solution(mesh):
    torus = Mesh(mesh.devices.reshape(4, 2, 4, 4), ("rows_0", "rows_1", "cols_0", "cols_1"))
    return jax.shard_map(
        shards,
        mesh=torus,
        in_specs=(
            P(ROWS, COLS),
            P(ROWS_COLS, None, None),
            P(ROWS_COLS, None),
            P(),
            P(),
            P(ROWS_COLS, None),
            P(ROWS_COLS),
        ),
        out_specs=(P(ROWS, COLS), P(ROWS_COLS), P()),
        check_vma=False,
    )
```

profile of v0, /device:TPU:96, one launch (start us, length us, event | category | flops | bytes accessed | tf_op | source)
XLA Modules:
  0.0 103.5 jit_solution(11161580845726467148)
XLA Ops:
  0.6 0.0 copy-start
  1.3 2.4 %pack.1 = bf16[16,80,384]{2,1,0:T(8,128)(2,1)} custom-call(s32[1]{0:T(128)S(6)} %copy.10.live_ref, bf16[768,384]{1,0:T(8,128)(2,1)} %dens_ref.1, f32[3,48,256]{2,1,0:T(8,128)} %bitcast.13, f32[48,256]{1,0:T(8,128)} %w_ref.1, s32[4,48]{1,0:T(4,128)} %bitcast.14), custom_call_target="tpu_custom_call" | custom-call | tf_op jit(solution)/shard_map/pack/pallas_call | solution.py:324
  3.7 7.0 %all-to-all-start = ((bf16[16,80,384]{2,1,0:T(8,128)(2,1)}), bf16[16,80,384]{2,1,0:T(8,128)(2,1)S(1)}, u32[]{:S(2)}, u32[]{:S(2)}) async-start(bf16[16,80,384]{2,1,0:T(8,128)(2,1)} %pack.1), calls=%async_computation | async-start | bytes 1966080 | tf_op jit(solution)/shard_map/all_to_all | solution.py:35
  10.8 16.9 %all-to-all-done.recv_ref = bf16[16,80,384]{2,1,0:T(8,128)(2,1)S(1)} async-done(((bf16[16,80,384]{2,1,0:T(8,128)(2,1)}), bf16[16,80,384]{2,1,0:T(8,128)(2,1)S(1)}, u32[]{:S(2)}, u32[]{:S(2)}) %all-to-all-start) | async-done | bytes 983072 | tf_op jit(solution)/shard_map/all_to_all | solution.py:35
  27.7 1.2 %broadcast_in_dim.10 = bf16[16,48,768]{2,1,0:T(8,128)(2,1)} broadcast(bf16[48,768]{1,0:T(8,128)(2,1)S(1)} %pad_maximum_fusion), dimensions={1,2} | broadcast | bytes 1253376 | tf_op jit(solution)/shard_map/broadcast_in_dim | solution.py:342
  28.9 3.7 %all-to-all-start.1 = ((bf16[16,48,768]{2,1,0:T(8,128)(2,1)}), bf16[16,48,768]{2,1,0:T(8,128)(2,1)S(1)}, u32[]{:S(2)}, u32[]{:S(2)}) async-start(bf16[16,48,768]{2,1,0:T(8,128)(2,1)} %broadcast_in_dim.10), calls=%async_computation.1 | async-start | bytes 2359296 | tf_op jit(solution)/shard_map/all_to_all | solution.py:35
  32.6 0.8 dynamic-slice_negate_fusion
  33.4 0.0 copy-done
  33.5 0.5 broadcast_in_dim.9.basis_ref
  34.0 10.4 %phi.1 = (bf16[48,512,256]{2,1,0:T(8,128)(2,1)}, s32[64]{0:T(128)S(1)}, f32[16,32,128]{2,1,0:T(8,128)S(1)}) custom-call(s32[16,48]{1,0:T(8,128)S(1)} %bitcast.12, bf16[16,80,384]{2,1,0:T(8,128)(2,1)S(1)} %all-to-all-done.recv_ref, f32[4,768,128]{2,1,0:T(8,128)S(1)} %broadcast_in_dim.9.basis_ref), custom_call_target="tpu_custom_call" | custom-call | flops 41943040 | bytes 16777216 | tf_op jit(solution)/shard_map/phi/pallas_call | solution.py:356
  44.4 5.0 %all-to-all-done.1 = bf16[16,48,768]{2,1,0:T(8,128)(2,1)S(1)} async-done(((bf16[16,48,768]{2,1,0:T(8,128)(2,1)}), bf16[16,48,768]{2,1,0:T(8,128)(2,1)S(1)}, u32[]{:S(2)}, u32[]{:S(2)}) %all-to-all-start.1) | async-done | bytes 1179680 | tf_op jit(solution)/shard_map/all_to_all | solution.py:35
  49.4 17.7 %xc.1 = (s16[16,304,128]{2,1,0:T(8,128)(2,1)}, f32[8,128]{1,0:T(8,128)S(1)}) custom-call(s32[64]{0:T(128)S(1)} %get-tuple-element.10.list_ref, bf16[768,768]{1,0:T(8,128)(2,1)S(1)} %bitcast.11, bf16[48,512,256]{2,1,0:T(8,128)(2,1)} %get-tuple-element.11.phi_ref, f32[16,32,128]{2,1,0:T(8,128)S(1)} %get-tuple-element.12.tile_ref), custom_call_target="tpu_custom_call" | custom-call | flops 8589934592 | bytes 16777216 | tf_op jit(solution)/shard_map/xc/pallas_call | solution.py:376
  67.1 4.4 %all-to-all-start.2 = ((s16[16,304,128]{2,1,0:T(8,128)(2,1)}), s16[16,304,128]{2,1,0:T(8,128)(2,1)S(1)}, u32[]{:S(2)}, u32[]{:S(2)}) async-start(s16[16,304,128]{2,1,0:T(8,128)(2,1)} %get-tuple-element.13), calls=%async_computation.2 | async-start | bytes 2490368 | tf_op jit(solution)/shard_map/all_to_all | solution.py:35
  71.5 1.9 %collective-permute-start.1 = (f32[8,128]{1,0:T(8,128)S(1)}, f32[8,128]{1,0:T(8,128)S(1)}, u32[]{:S(2)}, u32[]{:S(2)}) collective-permute-start(f32[8,128]{1,0:T(8,128)S(1)} %get-tuple-element.16), channel_id=1, source_target_pairs={{0,4},{4,8},{8,12},{12,0},{1,5},{5,9},{9,13},{13,1},{2,6},{6,10},{... | collective-permute-start | bytes 12296 | tf_op jit(solution)/shard_map/ppermute | solution.py:311
  73.5 1.4 %collective-permute-start.2 = (f32[8,128]{1,0:T(8,128)S(1)}, f32[8,128]{1,0:T(8,128)S(1)}, u32[]{:S(2)}, u32[]{:S(2)}) collective-permute-start(f32[8,128]{1,0:T(8,128)S(1)} %get-tuple-element.16), channel_id=1, source_target_pairs={{0,12},{4,0},{8,4},{12,8},{1,13},{5,1},{9,5},{13,9},{2,14},{6,2},{... | collective-permute-start | bytes 12296 | tf_op jit(solution)/shard_map/ppermute | solution.py:311
  74.8 2.2 %collective-permute-start = (f32[8,128]{1,0:T(8,128)S(1)}, f32[8,128]{1,0:T(8,128)S(1)}, u32[]{:S(2)}, u32[]{:S(2)}) collective-permute-start(f32[8,128]{1,0:T(8,128)S(1)} %get-tuple-element.16), channel_id=1, source_target_pairs={{0,8},{4,12},{8,0},{12,4},{1,9},{5,13},{9,1},{13,5},{2,10},{6,14},... | collective-permute-start | bytes 12296 | tf_op jit(solution)/shard_map/ppermute | solution.py:311
  77.0 5.1 %collective-permute-done.1 = f32[8,128]{1,0:T(8,128)S(1)} collective-permute-done((f32[8,128]{1,0:T(8,128)S(1)}, f32[8,128]{1,0:T(8,128)S(1)}, u32[]{:S(2)}, u32[]{:S(2)}) %collective-permute-start.1) | collective-permute-done | bytes 4128 | tf_op jit(solution)/shard_map/ppermute | solution.py:311
  82.1 0.3 collective-permute-done.2
  82.4 1.5 %collective-permute-done = f32[8,128]{1,0:T(8,128)S(1)} collective-permute-done((f32[8,128]{1,0:T(8,128)S(1)}, f32[8,128]{1,0:T(8,128)S(1)}, u32[]{:S(2)}, u32[]{:S(2)}) %collective-permute-start) | collective-permute-done | bytes 4128 | tf_op jit(solution)/shard_map/ppermute | solution.py:311
  83.9 0.0 collective-permute-start.3
  83.9 1.2 %collective-permute-done.3 = f32[8,128]{1,0:T(8,128)S(1)} collective-permute-done((f32[8,128]{1,0:T(8,128)S(1)}, f32[8,128]{1,0:T(8,128)S(1)}, u32[]{:S(2)}, u32[]{:S(2)}) %collective-permute-start.3) | collective-permute-done | bytes 4128 | tf_op jit(solution)/shard_map/ppermute | solution.py:316
  85.1 0.4 collective-permute-start.4
  85.4 3.3 %collective-permute-done.4 = f32[8,128]{1,0:T(8,128)S(1)} collective-permute-done((f32[8,128]{1,0:T(8,128)S(1)}, f32[8,128]{1,0:T(8,128)S(1)}, u32[]{:S(2)}, u32[]{:S(2)}) %collective-permute-start.4) | collective-permute-done | bytes 4128 | tf_op jit(solution)/shard_map/ppermute | solution.py:316
  88.7 0.0 collective-permute-start.5
  88.7 4.8 %collective-permute-done.5 = f32[8,128]{1,0:T(8,128)S(1)} collective-permute-done((f32[8,128]{1,0:T(8,128)S(1)}, f32[8,128]{1,0:T(8,128)S(1)}, u32[]{:S(2)}, u32[]{:S(2)}) %collective-permute-start.5) | collective-permute-done | bytes 4128 | tf_op jit(solution)/shard_map/ppermute | solution.py:316
  93.5 1.5 %collective-permute-start.6 = (f32[8,128]{1,0:T(8,128)S(1)}, f32[8,128]{1,0:T(8,128)S(1)}, u32[]{:S(2)}, u32[]{:S(2)}) collective-permute-start(f32[8,128]{1,0:T(8,128)S(1)} %add.60), channel_id=1, source_target_pairs={{0,1},{1,0},{2,3},{3,2},{4,5},{5,4},{6,7},{7,6},{8,9},{9,8},{10,11... | collective-permute-start | bytes 12296 | tf_op jit(solution)/shard_map/ppermute | solution.py:316
  95.0 2.1 %collective-permute-done.6 = f32[8,128]{1,0:T(8,128)S(1)} collective-permute-done((f32[8,128]{1,0:T(8,128)S(1)}, f32[8,128]{1,0:T(8,128)S(1)}, u32[]{:S(2)}, u32[]{:S(2)}) %collective-permute-start.6) | collective-permute-done | bytes 4128 | tf_op jit(solution)/shard_map/ppermute | solution.py:316
  97.1 2.8 %collective-permute-start.7 = (f32[8,128]{1,0:T(8,128)S(1)}, f32[8,128]{1,0:T(8,128)S(1)}, u32[]{:S(2)}, u32[]{:S(2)}) collective-permute-start(f32[8,128]{1,0:T(8,128)S(1)} %add.61), channel_id=1, source_target_pairs={{0,3},{1,2},{2,1},{3,0},{4,7},{5,6},{6,5},{7,4},{8,11},{9,10},{10,... | collective-permute-start | bytes 12296 | tf_op jit(solution)/shard_map/ppermute | solution.py:316
  99.9 2.1 %collective-permute-done.7 = f32[8,128]{1,0:T(8,128)S(1)} collective-permute-done((f32[8,128]{1,0:T(8,128)S(1)}, f32[8,128]{1,0:T(8,128)S(1)}, u32[]{:S(2)}, u32[]{:S(2)}) %collective-permute-start.7) | collective-permute-done | bytes 4128 | tf_op jit(solution)/shard_map/ppermute | solution.py:316
  101.9 0.5 slice.35
  102.5 0.0 all-to-all-done.2.recv_ref
  102.5 1.0 merge.1
  (13 shorter events, 0.1 us)
Async XLA Ops:
  0.6 32.8 %copy-start = (f32[3,6144]{1,0:T(4,128)S(1)}, f32[3,6144]{1,0:T(4,128)}, u32[]{:S(2)}) copy-start(f32[3,6144]{1,0:T(4,128)} %param.10) | copy-start | bytes 221188
  3.7 24.0 %all-to-all-start = ((bf16[16,80,384]{2,1,0:T(8,128)(2,1)}), bf16[16,80,384]{2,1,0:T(8,128)(2,1)S(1)}, u32[]{:S(2)}, u32[]{:S(2)}) async-start(bf16[16,80,384]{2,1,0:T(8,128)(2,1)} %pack.1), calls=%async_computation | async-start | bytes 1966080 | tf_op jit(solution)/shard_map/all_to_all | solution.py:35
  28.9 20.5 %all-to-all-start.1 = ((bf16[16,48,768]{2,1,0:T(8,128)(2,1)}), bf16[16,48,768]{2,1,0:T(8,128)(2,1)S(1)}, u32[]{:S(2)}, u32[]{:S(2)}) async-start(bf16[16,48,768]{2,1,0:T(8,128)(2,1)} %broadcast_in_dim.10), calls=%async_computation.1 | async-start | bytes 2359296 | tf_op jit(solution)/shard_map/all_to_all | solution.py:35
  67.1 35.4 %all-to-all-start.2 = ((s16[16,304,128]{2,1,0:T(8,128)(2,1)}), s16[16,304,128]{2,1,0:T(8,128)(2,1)S(1)}, u32[]{:S(2)}, u32[]{:S(2)}) async-start(s16[16,304,128]{2,1,0:T(8,128)(2,1)} %get-tuple-element.13), calls=%async_computation.2 | async-start | bytes 2490368 | tf_op jit(solution)/shard_map/all_to_all | solution.py:35
  71.5 10.6 %collective-permute-start.1 = (f32[8,128]{1,0:T(8,128)S(1)}, f32[8,128]{1,0:T(8,128)S(1)}, u32[]{:S(2)}, u32[]{:S(2)}) collective-permute-start(f32[8,128]{1,0:T(8,128)S(1)} %get-tuple-element.16), channel_id=1, source_target_pairs={{0,4},{4,8},{8,12},{12,0},{1,5},{5,9},{9,13},{13,1},{2,6},{6,10},{... | collective-permute-start | bytes 12296 | tf_op jit(solution)/shard_map/ppermute | solution.py:311
  73.5 9.0 %collective-permute-start.2 = (f32[8,128]{1,0:T(8,128)S(1)}, f32[8,128]{1,0:T(8,128)S(1)}, u32[]{:S(2)}, u32[]{:S(2)}) collective-permute-start(f32[8,128]{1,0:T(8,128)S(1)} %get-tuple-element.16), channel_id=1, source_target_pairs={{0,12},{4,0},{8,4},{12,8},{1,13},{5,1},{9,5},{13,9},{2,14},{6,2},{... | collective-permute-start | bytes 12296 | tf_op jit(solution)/shard_map/ppermute | solution.py:311
  74.8 9.1 %collective-permute-start = (f32[8,128]{1,0:T(8,128)S(1)}, f32[8,128]{1,0:T(8,128)S(1)}, u32[]{:S(2)}, u32[]{:S(2)}) collective-permute-start(f32[8,128]{1,0:T(8,128)S(1)} %get-tuple-element.16), channel_id=1, source_target_pairs={{0,8},{4,12},{8,0},{12,4},{1,9},{5,13},{9,1},{13,5},{2,10},{6,14},... | collective-permute-start | bytes 12296 | tf_op jit(solution)/shard_map/ppermute | solution.py:311
  83.9 1.2 %collective-permute-start.3 = (f32[8,128]{1,0:T(8,128)S(1)}, f32[8,128]{1,0:T(8,128)S(1)}, u32[]{:S(2)}, u32[]{:S(2)}) collective-permute-start(f32[8,128]{1,0:T(8,128)S(1)} %add_add_fusion), channel_id=1, source_target_pairs={{0,16},{16,0},{1,17},{17,1},{2,18},{18,2},{3,19},{19,3},{4,20},{20... | collective-permute-start | bytes 12296 | tf_op jit(solution)/shard_map/ppermute | solution.py:316
  85.1 3.6 %collective-permute-start.4 = (f32[8,128]{1,0:T(8,128)S(1)}, f32[8,128]{1,0:T(8,128)S(1)}, u32[]{:S(2)}, u32[]{:S(2)}) collective-permute-start(f32[8,128]{1,0:T(8,128)S(1)} %add.58), channel_id=1, source_target_pairs={{0,32},{32,0},{64,96},{96,64},{1,33},{33,1},{65,97},{97,65},{2,34}... | collective-permute-start | bytes 12296 | tf_op jit(solution)/shard_map/ppermute | solution.py:316
  88.7 4.8 %collective-permute-start.5 = (f32[8,128]{1,0:T(8,128)S(1)}, f32[8,128]{1,0:T(8,128)S(1)}, u32[]{:S(2)}, u32[]{:S(2)}) collective-permute-start(f32[8,128]{1,0:T(8,128)S(1)} %add.59), channel_id=1, source_target_pairs={{0,96},{32,64},{64,32},{96,0},{1,97},{33,65},{65,33},{97,1},{2,98}... | collective-permute-start | bytes 12296 | tf_op jit(solution)/shard_map/ppermute | solution.py:316
  93.5 3.6 %collective-permute-start.6 = (f32[8,128]{1,0:T(8,128)S(1)}, f32[8,128]{1,0:T(8,128)S(1)}, u32[]{:S(2)}, u32[]{:S(2)}) collective-permute-start(f32[8,128]{1,0:T(8,128)S(1)} %add.60), channel_id=1, source_target_pairs={{0,1},{1,0},{2,3},{3,2},{4,5},{5,4},{6,7},{7,6},{8,9},{9,8},{10,11... | collective-permute-start | bytes 12296 | tf_op jit(solution)/shard_map/ppermute | solution.py:316
  97.1 4.8 %collective-permute-start.7 = (f32[8,128]{1,0:T(8,128)S(1)}, f32[8,128]{1,0:T(8,128)S(1)}, u32[]{:S(2)}, u32[]{:S(2)}) collective-permute-start(f32[8,128]{1,0:T(8,128)S(1)} %add.61), channel_id=1, source_target_pairs={{0,3},{1,2},{2,1},{3,0},{4,7},{5,6},{6,5},{7,4},{8,11},{9,10},{10,... | collective-permute-start | bytes 12296 | tf_op jit(solution)/shard_map/ppermute | solution.py:316
where the time goes:
time: 105 us; the launch traced here: 103 us
  waiting for transfers between devices  42.2 us (40%)
  Pallas kernels  31.6 us (30%)
  starting transfers between devices  25.2 us (24%)
  local copies, waits for them, and re-layouts  2.16 us (2%)
  between operations  1.43 us (1%)
    all_to_all x3, waiting for transfers between devices, exchange(): return lax.all_to_all(blocks, COLS, split_axis=0, concat_axis=0, tiled=True)  21.9 us
    pallas_call x1, Pallas kernels, shards(): pl.pallas_call(xc_kernel, out_shape=(jax.ShapeDtypeStruct((NCOLS, SPAN *...  17.7 us
    all_to_all x3, starting transfers between devices, exchange(): return lax.all_to_all(blocks, COLS, split_axis=0, concat_axis=0, tiled=True)  15.2 us
    ppermute x5, waiting for transfers between devices, over_all(): lax.ppermute(value, axis, [(a, a ^ other) for a in range(lax.axis_size(ax...  13.4 us
    pallas_call x1, Pallas kernels, shards(): pl.pallas_call(phi_kernel, out_shape=(jax.ShapeDtypeStruct((SLOTS, NSIG *...  10.4 us
    ppermute x3, waiting for transfers between devices, over_all(): lax.ppermute(value, 'cols_0', [(a, (a + hop) % 4) for a in range(4)])  6.91 us
    ppermute x3, starting transfers between devices, over_all(): lax.ppermute(value, 'cols_0', [(a, (a + hop) % 4) for a in range(4)])  5.46 us
    ppermute x5, starting transfers between devices, over_all(): lax.ppermute(value, axis, [(a, a ^ other) for a in range(lax.axis_size(ax...  4.59 us
  transfers between devices with their start and end apart: 11, of which 10 were waited for; matrix products, arithmetic and copies ran while one was open for 2% of the time, Pallas kernels for 10%

commit v1 on v0

--- a/solution.py
+++ b/solution.py
@@ -82,6 +82,14 @@
             out_ref[d, STRIP:, q * 128 : (q + 1) * 128] = part
     for copy in strips:
         copy.wait()
+
+
+def strip_kernel(recv_ref, out_ref):
+    first = 2 * (2 * lax.axis_index("rows_0") + lax.axis_index("rows_1"))
+    for q in range(2):
+        half = recv_ref[first + q, :STRIP, :]
+        for d in range(NCOLS):
+            out_ref[d, :, q * 384 : (q + 1) * 384] = half
 
 
 def phi_kernel(meta_ref, recv_ref, basis_ref, phi_ref, list_ref, tile_ref, ring_s, sem):
@@ -337,9 +345,15 @@
     )(live_count, density, points.transpose(1, 0, 2), grid_weights, sig_blocks.T)
     recv = exchange(packed)
 
-    pair = lax.dynamic_slice(recv, (group * 2, 0, 0), (2, STRIP, 384))
-    strip = jnp.concatenate([pair[0], pair[1]], axis=1)
-    dens = exchange(jnp.broadcast_to(strip[None], (NCOLS, STRIP, OWN))).reshape(OWN, OWN)
+    strips = pl.pallas_call(
+        strip_kernel,
+        out_shape=jax.ShapeDtypeStruct((NCOLS, STRIP, OWN), jnp.bfloat16),
+        in_specs=[VMEM],
+        out_specs=VMEM,
+        compiler_params=pltpu.CompilerParams(vmem_limit_bytes=16 << 20),
+        name="strip",
+    )(recv)
+    dens = exchange(strips).reshape(OWN, OWN)
 
     tags = recv[:, STRIP + 24 : STRIP + 29, :SLOTS].astype(jnp.int32)
     meta = tags[:, 0] + 8 * tags[:, 1] + 64 * tags[:, 2] + 512 * tags[:, 3]

time: 105 us -> 105 us (level)
  blocking collectives: 0 us -> 23.2 us
  waiting for transfers between devices: 42.2 us -> 25.1 us
  starting transfers between devices: 25.2 us -> 19.1 us
  Pallas kernels: 31.6 us -> 32.8 us
  local copies, waits for them, and re-layouts: 2.16 us -> 0.99 us
    all_to_all x0 -> x1, blocking collectives: none -> 23.2 us  [exchange(): return lax.all_to_all(blocks, COLS, split_axis=0, concat_axis=0, tiled=True)]
    all_to_all x3 -> x2, waiting for transfers between devices: 21.9 us -> 6.06 us  [exchange(): return lax.all_to_all(blocks, COLS, split_axis=0, concat_axis=0, tiled=True)]
    all_to_all x3 -> x2, starting transfers between devices: 15.2 us -> 7.86 us  [exchange(): return lax.all_to_all(blocks, COLS, split_axis=0, concat_axis=0, tiled=True)]
    ppermute x3, waiting for transfers between devices: 6.91 us -> 5.53 us  [over_all(): lax.ppermute(value, 'cols_0', [(a, (a + hop) % 4) for a in range(4)])]
    ppermute x3, starting transfers between devices: 5.46 us -> 6.67 us  [over_all(): lax.ppermute(value, 'cols_0', [(a, (a + hop) % 4) for a in range(4)])]
    pallas_call x0 -> x1, Pallas kernels: none -> 1.19 us  [shards(): pl.pallas_call(strip_kernel, out_shape=jax.ShapeDtypeStruct((NCOLS, STRIP...]
    broadcast_in_dim x1 -> x0, local copies, waits for them, and re-layouts: 1.16 us -> none  [shards(): jnp.broadcast_to(strip[None], (NCOLS, STRIP, OWN))]
  transfers between devices with their start and end apart: 11 -> 10, of which waited for: 10 -> 7; matrix products, arithmetic and copies ran while one was open for 2% -> 2% of each run, Pallas kernels for 10% -> 10%
where the time goes in v1:
time: 105 us; the launch traced here: 103 us
  Pallas kernels  32.8 us (31%)
  waiting for transfers between devices  25.1 us (24%)
  blocking collectives  23.2 us (22%)
  starting transfers between devices  19.1 us (18%)
  between operations  1.42 us (1%)
    all_to_all x1, blocking collectives, exchange(): return lax.all_to_all(blocks, COLS, split_axis=0, concat_axis=0, tiled=True)  23.2 us
    pallas_call x1, Pallas kernels, shards(): pl.pallas_call(xc_kernel, out_shape=(jax.ShapeDtypeStruct((NCOLS, SPAN *...  17.7 us
    ppermute x5, waiting for transfers between devices, over_all(): lax.ppermute(value, axis, [(a, a ^ other) for a in range(lax.axis_size(ax...  13.5 us
    pallas_call x1, Pallas kernels, shards(): pl.pallas_call(phi_kernel, out_shape=(jax.ShapeDtypeStruct((SLOTS, NSIG *...  10.5 us
    all_to_all x2, starting transfers between devices, exchange(): return lax.all_to_all(blocks, COLS, split_axis=0, concat_axis=0, tiled=True)  7.86 us
    ppermute x3, starting transfers between devices, over_all(): lax.ppermute(value, 'cols_0', [(a, (a + hop) % 4) for a in range(4)])  6.67 us
    all_to_all x2, waiting for transfers between devices, exchange(): return lax.all_to_all(blocks, COLS, split_axis=0, concat_axis=0, tiled=True)  6.06 us
    ppermute x3, waiting for transfers between devices, over_all(): lax.ppermute(value, 'cols_0', [(a, (a + hop) % 4) for a in range(4)])  5.53 us
  transfers between devices with their start and end apart: 10, of which 7 were waited for; matrix products, arithmetic and copies ran while one was open for 2% of the time, Pallas kernels for 10%

profile of v1, /device:TPU:96, one launch (start us, length us, event | category | flops | bytes accessed | tf_op | source)
XLA Modules:
  0.0 103.4 jit_solution(8187703015275737014)
XLA Ops:
  0.6 0.0 copy-start
  1.3 2.4 %pack.1 = bf16[16,80,384]{2,1,0:T(8,128)(2,1)} custom-call(s32[1]{0:T(128)S(6)} %copy.10.live_ref, bf16[768,384]{1,0:T(8,128)(2,1)} %dens_ref.1, f32[3,48,256]{2,1,0:T(8,128)} %bitcast.9, f32[48,256]{1,0:T(8,128)} %w_ref.1, s32[4,48]{1,0:T(4,128)} %bitcast.10), custom_call_target="tpu_custom_call" | custom-call | tf_op jit(solution)/shard_map/pack/pallas_call | solution.py:332
  3.7 23.2 %all_to_all.15.recv_ref = bf16[16,80,384]{2,1,0:T(8,128)(2,1)S(1)} all-to-all(bf16[16,80,384]{2,1,0:T(8,128)(2,1)} %pack.1), channel_id=1, replica_groups=mesh['rows_0'=4,'rows_1'=2,'cols_0'=4,'cols_1'=4] {'cols_0','cols_1'}, dimensions={0} | all-to-all | bytes 1966080 | tf_op jit(solution)/shard_map/all_to_all | solution.py:35
  26.9 1.2 %strip.1 = bf16[16,48,768]{2,1,0:T(8,128)(2,1)} custom-call(bf16[16,80,384]{2,1,0:T(8,128)(2,1)S(1)} %all_to_all.15.recv_ref), custom_call_target="tpu_custom_call" | custom-call | tf_op jit(solution)/shard_map/strip/pallas_call | solution.py:348
  28.1 3.8 %all-to-all-start.1 = ((bf16[16,48,768]{2,1,0:T(8,128)(2,1)}), bf16[16,48,768]{2,1,0:T(8,128)(2,1)S(1)}, u32[]{:S(2)}, u32[]{:S(2)}) async-start(bf16[16,48,768]{2,1,0:T(8,128)(2,1)} %strip.1), calls=%async_computation.1 | async-start | bytes 2359296 | tf_op jit(solution)/shard_map/all_to_all | solution.py:35
  31.9 0.8 dynamic-slice_negate_fusion
  32.7 0.0 copy-done
  32.8 0.5 broadcast_in_dim.12.basis_ref
  33.3 10.5 %phi.1 = (bf16[48,512,256]{2,1,0:T(8,128)(2,1)}, s32[64]{0:T(128)S(1)}, f32[16,32,128]{2,1,0:T(8,128)S(1)}) custom-call(s32[16,48]{1,0:T(8,128)S(1)} %bitcast.8, bf16[16,80,384]{2,1,0:T(8,128)(2,1)S(1)} %all_to_all.15.recv_ref, f32[4,768,128]{2,1,0:T(8,128)S(1)} %broadcast_in_dim.12.basis_ref), custom_call_target="tpu_custom_call" | custom-call | flops 41943040 | bytes 16777216 | tf_op jit(solution)/shard_map/phi/pallas_call | solution.py:370
  43.7 6.1 %all-to-all-done.1 = bf16[16,48,768]{2,1,0:T(8,128)(2,1)S(1)} async-done(((bf16[16,48,768]{2,1,0:T(8,128)(2,1)}), bf16[16,48,768]{2,1,0:T(8,128)(2,1)S(1)}, u32[]{:S(2)}, u32[]{:S(2)}) %all-to-all-start.1) | async-done | bytes 1179680 | tf_op jit(solution)/shard_map/all_to_all | solution.py:35
  49.8 17.7 %xc.1 = (s16[16,304,128]{2,1,0:T(8,128)(2,1)}, f32[8,128]{1,0:T(8,128)S(1)}) custom-call(s32[64]{0:T(128)S(1)} %get-tuple-element.10.list_ref, bf16[768,768]{1,0:T(8,128)(2,1)S(1)} %bitcast.7, bf16[48,512,256]{2,1,0:T(8,128)(2,1)} %get-tuple-element.11.phi_ref, f32[16,32,128]{2,1,0:T(8,128)S(1)} %get-tuple-element.12.tile_ref), custom_call_target="tpu_custom_call" | custom-call | flops 8589934592 | bytes 16777216 | tf_op jit(solution)/shard_map/xc/pallas_call | solution.py:390
  67.5 4.1 %all-to-all-start.2 = ((s16[16,304,128]{2,1,0:T(8,128)(2,1)}), s16[16,304,128]{2,1,0:T(8,128)(2,1)S(1)}, u32[]{:S(2)}, u32[]{:S(2)}) async-start(s16[16,304,128]{2,1,0:T(8,128)(2,1)} %get-tuple-element.13), calls=%async_computation.2 | async-start | bytes 2490368 | tf_op jit(solution)/shard_map/all_to_all | solution.py:35
  71.6 3.4 %collective-permute-start = (f32[8,128]{1,0:T(8,128)S(1)}, f32[8,128]{1,0:T(8,128)S(1)}, u32[]{:S(2)}, u32[]{:S(2)}) collective-permute-start(f32[8,128]{1,0:T(8,128)S(1)} %get-tuple-element.16), channel_id=1, source_target_pairs={{0,8},{4,12},{8,0},{12,4},{1,9},{5,13},{9,1},{13,5},{2,10},{6,14},... | collective-permute-start | bytes 12296 | tf_op jit(solution)/shard_map/ppermute | solution.py:319
  75.0 0.6 collective-permute-start.1
  75.6 2.7 %collective-permute-start.2 = (f32[8,128]{1,0:T(8,128)S(1)}, f32[8,128]{1,0:T(8,128)S(1)}, u32[]{:S(2)}, u32[]{:S(2)}) collective-permute-start(f32[8,128]{1,0:T(8,128)S(1)} %get-tuple-element.16), channel_id=1, source_target_pairs={{0,12},{4,0},{8,4},{12,8},{1,13},{5,1},{9,5},{13,9},{2,14},{6,2},{... | collective-permute-start | bytes 12296 | tf_op jit(solution)/shard_map/ppermute | solution.py:319
  78.3 5.5 %collective-permute-done = f32[8,128]{1,0:T(8,128)S(1)} collective-permute-done((f32[8,128]{1,0:T(8,128)S(1)}, f32[8,128]{1,0:T(8,128)S(1)}, u32[]{:S(2)}, u32[]{:S(2)}) %collective-permute-start) | collective-permute-done | bytes 4128 | tf_op jit(solution)/shard_map/ppermute | solution.py:319
  83.8 0.0 collective-permute-done.1
  83.8 0.0 collective-permute-done.2
  83.8 0.1 collective-permute-start.3
  83.9 1.2 %collective-permute-done.3 = f32[8,128]{1,0:T(8,128)S(1)} collective-permute-done((f32[8,128]{1,0:T(8,128)S(1)}, f32[8,128]{1,0:T(8,128)S(1)}, u32[]{:S(2)}, u32[]{:S(2)}) %collective-permute-start.3) | collective-permute-done | bytes 4128 | tf_op jit(solution)/shard_map/ppermute | solution.py:324
  85.1 0.3 collective-permute-start.4
  85.4 3.3 %collective-permute-done.4 = f32[8,128]{1,0:T(8,128)S(1)} collective-permute-done((f32[8,128]{1,0:T(8,128)S(1)}, f32[8,128]{1,0:T(8,128)S(1)}, u32[]{:S(2)}, u32[]{:S(2)}) %collective-permute-start.4) | collective-permute-done | bytes 4128 | tf_op jit(solution)/shard_map/ppermute | solution.py:324
  88.7 0.0 collective-permute-start.5
  88.7 4.8 %collective-permute-done.5 = f32[8,128]{1,0:T(8,128)S(1)} collective-permute-done((f32[8,128]{1,0:T(8,128)S(1)}, f32[8,128]{1,0:T(8,128)S(1)}, u32[]{:S(2)}, u32[]{:S(2)}) %collective-permute-start.5) | collective-permute-done | bytes 4128 | tf_op jit(solution)/shard_map/ppermute | solution.py:324
  93.5 1.5 %collective-permute-start.6 = (f32[8,128]{1,0:T(8,128)S(1)}, f32[8,128]{1,0:T(8,128)S(1)}, u32[]{:S(2)}, u32[]{:S(2)}) collective-permute-start(f32[8,128]{1,0:T(8,128)S(1)} %add.56), channel_id=1, source_target_pairs={{0,1},{1,0},{2,3},{3,2},{4,5},{5,4},{6,7},{7,6},{8,9},{9,8},{10,11... | collective-permute-start | bytes 12296 | tf_op jit(solution)/shard_map/ppermute | solution.py:324
  95.0 2.1 %collective-permute-done.6 = f32[8,128]{1,0:T(8,128)S(1)} collective-permute-done((f32[8,128]{1,0:T(8,128)S(1)}, f32[8,128]{1,0:T(8,128)S(1)}, u32[]{:S(2)}, u32[]{:S(2)}) %collective-permute-start.6) | collective-permute-done | bytes 4128 | tf_op jit(solution)/shard_map/ppermute | solution.py:324
  97.1 2.7 %collective-permute-start.7 = (f32[8,128]{1,0:T(8,128)S(1)}, f32[8,128]{1,0:T(8,128)S(1)}, u32[]{:S(2)}, u32[]{:S(2)}) collective-permute-start(f32[8,128]{1,0:T(8,128)S(1)} %add.57), channel_id=1, source_target_pairs={{0,3},{1,2},{2,1},{3,0},{4,7},{5,6},{6,5},{7,4},{8,11},{9,10},{10,... | collective-permute-start | bytes 12296 | tf_op jit(solution)/shard_map/ppermute | solution.py:324
  99.8 2.1 %collective-permute-done.7 = f32[8,128]{1,0:T(8,128)S(1)} collective-permute-done((f32[8,128]{1,0:T(8,128)S(1)}, f32[8,128]{1,0:T(8,128)S(1)}, u32[]{:S(2)}, u32[]{:S(2)}) %collective-permute-start.7) | collective-permute-done | bytes 4128 | tf_op jit(solution)/shard_map/ppermute | solution.py:324
  101.9 0.5 slice.27
  102.4 0.0 all-to-all-done.2.recv_ref
  102.4 1.0 merge.1
  (11 shorter events, 0.1 us)
Async XLA Ops:
  0.6 32.1 %copy-start = (f32[3,6144]{1,0:T(4,128)S(1)}, f32[3,6144]{1,0:T(4,128)}, u32[]{:S(2)}) copy-start(f32[3,6144]{1,0:T(4,128)} %param.10) | copy-start | bytes 221188
  28.1 21.7 %all-to-all-start.1 = ((bf16[16,48,768]{2,1,0:T(8,128)(2,1)}), bf16[16,48,768]{2,1,0:T(8,128)(2,1)S(1)}, u32[]{:S(2)}, u32[]{:S(2)}) async-start(bf16[16,48,768]{2,1,0:T(8,128)(2,1)} %strip.1), calls=%async_computation.1 | async-start | bytes 2359296 | tf_op jit(solution)/shard_map/all_to_all | solution.py:35
  67.5 34.9 %all-to-all-start.2 = ((s16[16,304,128]{2,1,0:T(8,128)(2,1)}), s16[16,304,128]{2,1,0:T(8,128)(2,1)S(1)}, u32[]{:S(2)}, u32[]{:S(2)}) async-start(s16[16,304,128]{2,1,0:T(8,128)(2,1)} %get-tuple-element.13), calls=%async_computation.2 | async-start | bytes 2490368 | tf_op jit(solution)/shard_map/all_to_all | solution.py:35
  71.6 12.2 %collective-permute-start = (f32[8,128]{1,0:T(8,128)S(1)}, f32[8,128]{1,0:T(8,128)S(1)}, u32[]{:S(2)}, u32[]{:S(2)}) collective-permute-start(f32[8,128]{1,0:T(8,128)S(1)} %get-tuple-element.16), channel_id=1, source_target_pairs={{0,8},{4,12},{8,0},{12,4},{1,9},{5,13},{9,1},{13,5},{2,10},{6,14},... | collective-permute-start | bytes 12296 | tf_op jit(solution)/shard_map/ppermute | solution.py:319
  75.0 8.8 %collective-permute-start.1 = (f32[8,128]{1,0:T(8,128)S(1)}, f32[8,128]{1,0:T(8,128)S(1)}, u32[]{:S(2)}, u32[]{:S(2)}) collective-permute-start(f32[8,128]{1,0:T(8,128)S(1)} %get-tuple-element.16), channel_id=1, source_target_pairs={{0,4},{4,8},{8,12},{12,0},{1,5},{5,9},{9,13},{13,1},{2,6},{6,10},{... | collective-permute-start | bytes 12296 | tf_op jit(solution)/shard_map/ppermute | solution.py:319
  75.6 8.2 %collective-permute-start.2 = (f32[8,128]{1,0:T(8,128)S(1)}, f32[8,128]{1,0:T(8,128)S(1)}, u32[]{:S(2)}, u32[]{:S(2)}) collective-permute-start(f32[8,128]{1,0:T(8,128)S(1)} %get-tuple-element.16), channel_id=1, source_target_pairs={{0,12},{4,0},{8,4},{12,8},{1,13},{5,1},{9,5},{13,9},{2,14},{6,2},{... | collective-permute-start | bytes 12296 | tf_op jit(solution)/shard_map/ppermute | solution.py:319
  83.8 1.2 %collective-permute-start.3 = (f32[8,128]{1,0:T(8,128)S(1)}, f32[8,128]{1,0:T(8,128)S(1)}, u32[]{:S(2)}, u32[]{:S(2)}) collective-permute-start(f32[8,128]{1,0:T(8,128)S(1)} %add_add_fusion), channel_id=1, source_target_pairs={{0,16},{16,0},{1,17},{17,1},{2,18},{18,2},{3,19},{19,3},{4,20},{20... | collective-permute-start | bytes 12296 | tf_op jit(solution)/shard_map/ppermute | solution.py:324
  85.1 3.6 %collective-permute-start.4 = (f32[8,128]{1,0:T(8,128)S(1)}, f32[8,128]{1,0:T(8,128)S(1)}, u32[]{:S(2)}, u32[]{:S(2)}) collective-permute-start(f32[8,128]{1,0:T(8,128)S(1)} %add.54), channel_id=1, source_target_pairs={{0,32},{32,0},{64,96},{96,64},{1,33},{33,1},{65,97},{97,65},{2,34}... | collective-permute-start | bytes 12296 | tf_op jit(solution)/shard_map/ppermute | solution.py:324
  88.7 4.8 %collective-permute-start.5 = (f32[8,128]{1,0:T(8,128)S(1)}, f32[8,128]{1,0:T(8,128)S(1)}, u32[]{:S(2)}, u32[]{:S(2)}) collective-permute-start(f32[8,128]{1,0:T(8,128)S(1)} %add.55), channel_id=1, source_target_pairs={{0,96},{32,64},{64,32},{96,0},{1,97},{33,65},{65,33},{97,1},{2,98}... | collective-permute-start | bytes 12296 | tf_op jit(solution)/shard_map/ppermute | solution.py:324
  93.5 3.6 %collective-permute-start.6 = (f32[8,128]{1,0:T(8,128)S(1)}, f32[8,128]{1,0:T(8,128)S(1)}, u32[]{:S(2)}, u32[]{:S(2)}) collective-permute-start(f32[8,128]{1,0:T(8,128)S(1)} %add.56), channel_id=1, source_target_pairs={{0,1},{1,0},{2,3},{3,2},{4,5},{5,4},{6,7},{7,6},{8,9},{9,8},{10,11... | collective-permute-start | bytes 12296 | tf_op jit(solution)/shard_map/ppermute | solution.py:324
  97.1 4.8 %collective-permute-start.7 = (f32[8,128]{1,0:T(8,128)S(1)}, f32[8,128]{1,0:T(8,128)S(1)}, u32[]{:S(2)}, u32[]{:S(2)}) collective-permute-start(f32[8,128]{1,0:T(8,128)S(1)} %add.57), channel_id=1, source_target_pairs={{0,3},{1,2},{2,1},{3,0},{4,7},{5,6},{6,5},{7,4},{8,11},{9,10},{10,... | collective-permute-start | bytes 12296 | tf_op jit(solution)/shard_map/ppermute | solution.py:324

commit v2 on v1

--- a/solution.py
+++ b/solution.py
@@ -152,7 +152,7 @@
 
 
 def xc_kernel(
-    list_ref, dens_ref, phi_ref, tile_ref, out_ref, total_ref,
+    list_ref, dens_ref, phi_ref, tile_ref, out_ref,
     dens_s, acc_s, scaled_s, image_s, factor_s, term_s, ring_s, sem,
 ):
     total = list_ref[63]
@@ -259,7 +259,11 @@
 
     me = column()
     terms = jnp.broadcast_to(jnp.sum(term_s[...], axis=1, keepdims=True), (NCOLS * 4, 128))
-    total_ref[...] = jnp.broadcast_to(jnp.sum(terms, axis=0, keepdims=True), total_ref.shape)
+    whole = jnp.sum(terms, axis=0, keepdims=True)
+    whole_code = quarter_octaves(jnp.abs(whole))
+    whole = whole * (TOP * jnp.exp2(-0.25 * whole_code))
+    whole_high = jnp.round(whole)
+    whole_low = (whole - whole_high) * (2.0 * TOP)
     peak = jnp.max(jnp.abs(terms), axis=0, keepdims=True)
     term_code = quarter_octaves(peak)
     terms = terms * (TOP * jnp.exp2(-0.25 * term_code))
@@ -284,7 +288,10 @@
         high = jnp.round(energy)
         low = (energy - high) * (2.0 * TOP)
         codes = jnp.sum(jnp.where(row == lane, code, 0.0), axis=0, keepdims=True)
-        extra = jnp.where(line == 0, high, jnp.where(line == 1, low, jnp.where(line == 2, codes, term_code)))
+        extra = jnp.zeros((EXTRA, 128), jnp.float32)
+        lines = (high, low, codes, term_code, whole_high, whole_low, whole_code)
+        for q, values in enumerate(lines):
+            extra = jnp.where(line == q, values, extra)
         out_ref[j, SPAN * STRIP :, :] = to_short(extra)
 
 
@@ -296,33 +303,30 @@
     return jnp.round(x).astype(jnp.int32).astype(jnp.int16)
 
 
-def merge_kernel(recv_ref, xc_ref, energy_ref):
+def merge_kernel(recv_ref, xc_ref, energy_ref, total_ref):
     row = lax.broadcasted_iota(jnp.int32, (STRIP, 128), 0)
     lane = lax.broadcasted_iota(jnp.int32, (STRIP, 128), 1)
-    energy = jnp.zeros((1, 128), jnp.float32)
+    energy = whole = jnp.zeros((1, 128), jnp.float32)
     total = [jnp.zeros((STRIP, 128), jnp.float32) for _ in range(SPAN)]
     for j in range(NCOLS):
         extra = recv_ref[j, SPAN * STRIP :, :].astype(jnp.int32).astype(jnp.float32)
-        unit = (1.0 / TOP) * jnp.exp2(0.25 * extra[2:4])
-        scale = jnp.sum(jnp.where(row == lane, unit[:1], 0.0), axis=1, keepdims=True)
+        unit = (1.0 / TOP) * jnp.exp2(0.25 * extra[:8])
+        scale = jnp.sum(jnp.where(row == lane, unit[2:3], 0.0), axis=1, keepdims=True)
         for b in range(SPAN):
             part = recv_ref[j, b * STRIP : (b + 1) * STRIP, :].astype(jnp.int32)
             total[b] = total[b] + part.astype(jnp.float32) * scale
-        energy = energy + (extra[:1] + extra[1:2] * (0.5 / TOP)) * unit[1:2]
+        energy = energy + (extra[:1] + extra[1:2] * (0.5 / TOP)) * unit[3:4]
+        whole = whole + (extra[4:5] + extra[5:6] * (0.5 / TOP)) * unit[6:7]
     for b in range(SPAN):
         xc_ref[:, b * BLOCK : (b + 1) * BLOCK] = total[b]
     energy_ref[...] = energy[:, :SLOTS]
-
-
-def over_all(value):
-    left, far, right = (
-        lax.ppermute(value, "cols_0", [(a, (a + hop) % 4) for a in range(4)])
-        for hop in (1, 2, 3)
-    )
-    value = (value + far) + (left + right)
-    for axis, other in (("rows_1", 1), ("rows_0", 1), ("rows_0", 3), ("cols_1", 1), ("cols_1", 3)):
-        moved = lax.ppermute(value, axis, [(a, a ^ other) for a in range(lax.axis_size(axis))])
-        value = value + moved
+    total_ref[...] = jnp.broadcast_to(whole, total_ref.shape)
+
+
+def over_rows(value):
+    for axis, other in (("rows_1", 1), ("rows_0", 1), ("rows_0", 3)):
+        pairs = [(a, a ^ other) for a in range(lax.axis_size(axis))]
+        value = value + lax.ppermute(value, axis, pairs)
     return value
 
 
@@ -387,14 +391,11 @@
         name="phi",
     )(meta, recv, basis)
 
-    contrib, total = pl.pallas_call(
+    contrib = pl.pallas_call(
         xc_kernel,
-        out_shape=(
-            jax.ShapeDtypeStruct((NCOLS, SPAN * STRIP + EXTRA, BLOCK), jnp.int16),
-            jax.ShapeDtypeStruct((8, 128), jnp.float32),
-        ),
+        out_shape=jax.ShapeDtypeStruct((NCOLS, SPAN * STRIP + EXTRA, BLOCK), jnp.int16),
         in_specs=[SMEM, VMEM, ANY, VMEM],
-        out_specs=(VMEM, VMEM),
+        out_specs=VMEM,
         scratch_shapes=[
             pltpu.VMEM((SPAN * SPAN, BLOCK, BLOCK), jnp.bfloat16),
             pltpu.VMEM((SPAN, OWN, BLOCK), jnp.float32),
@@ -413,19 +414,20 @@
     )(batches, dens, phi, tiles)
 
     parts = exchange(contrib)
-    exc_total = over_all(total)[0, 0]
     merge = pl.pallas_call(
         merge_kernel,
         out_shape=(
             jax.ShapeDtypeStruct((STRIP, OWN), jnp.float32),
             jax.ShapeDtypeStruct((1, SLOTS), jnp.float32),
+            jax.ShapeDtypeStruct((8, 128), jnp.float32),
         ),
         in_specs=[VMEM],
-        out_specs=(VMEM, VMEM),
+        out_specs=(VMEM, VMEM, VMEM),
         compiler_params=pltpu.CompilerParams(vmem_limit_bytes=16 << 20),
         name="merge",
     )
-    xc_rows, energy = merge(parts)
+    xc_rows, energy, total = merge(parts)
+    exc_total = over_rows(total)[0, 0]
     return (xc_rows.T, energy.reshape(SLOTS), exc_total)
 
 

time: 105 us -> 96.6 us (0.920)
  blocking collectives: 23.2 us -> 41 us
  starting transfers between devices: 19.1 us -> 4.08 us
  waiting for transfers between devices: 25.1 us -> 15.4 us
  Pallas kernels: 32.8 us -> 31.6 us
    all_to_all x1 -> x2, blocking collectives: 23.2 us -> 41 us  [exchange(): return lax.all_to_all(blocks, COLS, split_axis=0, concat_axis=0, tiled=True)]
    ppermute x8 -> x3, starting transfers between devices: 11.2 us -> 0.28 us  [over_rows(): value = value + lax.ppermute(value, axis, pairs)]
    ppermute x8 -> x3, waiting for transfers between devices: 19 us -> 9.31 us  [over_rows(): value = value + lax.ppermute(value, axis, pairs)]
    all_to_all x2 -> x1, starting transfers between devices: 7.86 us -> 3.8 us  [exchange(): return lax.all_to_all(blocks, COLS, split_axis=0, concat_axis=0, tiled=True)]
    pallas_call x2, Pallas kernels: 18.7 us -> 17.6 us  [the longest x1 16.6 us: shards(): pl.pallas_call(xc_kernel, out_shape=jax.ShapeDtypeStruct((NCOLS, SPAN * S...]
    all_to_all x2 -> x1, waiting for transfers between devices: 6.06 us -> 6.07 us  [exchange(): return lax.all_to_all(blocks, COLS, split_axis=0, concat_axis=0, tiled=True)]
  transfers between devices with their start and end apart: 10 -> 4, of which waited for: 7 -> 4; matrix products, arithmetic and copies ran while one was open for 2% -> 1% of each run, Pallas kernels for 10% -> 11%
where the time goes in v2:
time: 96.6 us; the launch traced here: 95.3 us
  blocking collectives  41 us (42%)
  Pallas kernels  31.6 us (33%)
  waiting for transfers between devices  15.4 us (16%)
  starting transfers between devices  4.08 us (4%)
  between operations  1.39 us (1%)
  local copies, waits for them, and re-layouts  0.99 us (1%)
    all_to_all x2, blocking collectives, exchange(): return lax.all_to_all(blocks, COLS, split_axis=0, concat_axis=0, tiled=True)  41 us
    pallas_call x1, Pallas kernels, shards(): pl.pallas_call(xc_kernel, out_shape=jax.ShapeDtypeStruct((NCOLS, SPAN * S...  16.6 us
    pallas_call x1, Pallas kernels, shards(): pl.pallas_call(phi_kernel, out_shape=(jax.ShapeDtypeStruct((SLOTS, NSIG *...  10.4 us
    ppermute x3, waiting for transfers between devices, over_rows(): value = value + lax.ppermute(value, axis, pairs)  9.31 us
    all_to_all x1, waiting for transfers between devices, exchange(): return lax.all_to_all(blocks, COLS, split_axis=0, concat_axis=0, tiled=True)  6.07 us
    all_to_all x1, starting transfers between devices, exchange(): return lax.all_to_all(blocks, COLS, split_axis=0, concat_axis=0, tiled=True)  3.8 us
    pallas_call x1, Pallas kernels, shards(): pl.pallas_call(pack_kernel, out_shape=jax.ShapeDtypeStruct((NCOLS, STRIP...  2.39 us
  transfers between devices with their start and end apart: 4, of which 4 were waited for; matrix products, arithmetic and copies ran while one was open for 1% of the time, Pallas kernels for 11%

profile of v2, /device:TPU:96, one launch (start us, length us, event | category | flops | bytes accessed | tf_op | source)
XLA Modules:
  0.0 95.3 jit_solution(10536831802223829074)
XLA Ops:
  0.6 0.0 copy-start
  1.3 2.4 %pack.1 = bf16[16,80,384]{2,1,0:T(8,128)(2,1)} custom-call(s32[1]{0:T(128)S(6)} %copy.10.live_ref, bf16[768,384]{1,0:T(8,128)(2,1)} %dens_ref.1, f32[3,48,256]{2,1,0:T(8,128)} %bitcast.9, f32[48,256]{1,0:T(8,128)} %w_ref.1, s32[4,48]{1,0:T(4,128)} %bitcast.10), custom_call_target="tpu_custom_call" | custom-call | tf_op jit(solution)/shard_map/pack/pallas_call | solution.py:336
  3.7 23.2 %all_to_all.15.recv_ref = bf16[16,80,384]{2,1,0:T(8,128)(2,1)S(1)} all-to-all(bf16[16,80,384]{2,1,0:T(8,128)(2,1)} %pack.1), channel_id=1, replica_groups=mesh['rows_0'=4,'rows_1'=2,'cols_0'=4,'cols_1'=4] {'cols_0','cols_1'}, dimensions={0} | all-to-all | bytes 1966080 | tf_op jit(solution)/shard_map/all_to_all | solution.py:35
  26.9 1.2 %strip.1 = bf16[16,48,768]{2,1,0:T(8,128)(2,1)} custom-call(bf16[16,80,384]{2,1,0:T(8,128)(2,1)S(1)} %all_to_all.15.recv_ref), custom_call_target="tpu_custom_call" | custom-call | tf_op jit(solution)/shard_map/strip/pallas_call | solution.py:352
  28.1 3.8 %all-to-all-start.1 = ((bf16[16,48,768]{2,1,0:T(8,128)(2,1)}), bf16[16,48,768]{2,1,0:T(8,128)(2,1)S(1)}, u32[]{:S(2)}, u32[]{:S(2)}) async-start(bf16[16,48,768]{2,1,0:T(8,128)(2,1)} %strip.1), calls=%async_computation.1 | async-start | bytes 2359296 | tf_op jit(solution)/shard_map/all_to_all | solution.py:35
  31.9 0.8 dynamic-slice_negate_fusion
  32.7 0.0 copy-done
  32.8 0.5 broadcast_in_dim.12.basis_ref
  33.3 10.4 %phi.1 = (bf16[48,512,256]{2,1,0:T(8,128)(2,1)}, s32[64]{0:T(128)S(1)}, f32[16,32,128]{2,1,0:T(8,128)S(1)}) custom-call(s32[16,48]{1,0:T(8,128)S(1)} %bitcast.8, bf16[16,80,384]{2,1,0:T(8,128)(2,1)S(1)} %all_to_all.15.recv_ref, f32[4,768,128]{2,1,0:T(8,128)S(1)} %broadcast_in_dim.12.basis_ref), custom_call_target="tpu_custom_call" | custom-call | flops 41943040 | bytes 16777216 | tf_op jit(solution)/shard_map/phi/pallas_call | solution.py:374
  43.7 6.1 %all-to-all-done.1 = bf16[16,48,768]{2,1,0:T(8,128)(2,1)S(1)} async-done(((bf16[16,48,768]{2,1,0:T(8,128)(2,1)}), bf16[16,48,768]{2,1,0:T(8,128)(2,1)S(1)}, u32[]{:S(2)}, u32[]{:S(2)}) %all-to-all-start.1) | async-done | bytes 1179680 | tf_op jit(solution)/shard_map/all_to_all | solution.py:35
  49.8 16.6 %xc.1 = s16[16,304,128]{2,1,0:T(8,128)(2,1)S(1)} custom-call(s32[64]{0:T(128)S(1)} %get-tuple-element.9.list_ref, bf16[768,768]{1,0:T(8,128)(2,1)S(1)} %bitcast.7, bf16[48,512,256]{2,1,0:T(8,128)(2,1)} %get-tuple-element.10.phi_ref, f32[16,32,128]{2,1,0:T(8,128)S(1)} %get-tuple-element.11.tile_ref), custom_call_target="tpu_custom_call" | custom-call | flops 8589934592 | bytes 16777216 | tf_op jit(solution)/shard_map/xc/pallas_call | solution.py:394
  66.4 17.8 %all_to_all.16.recv_ref = s16[16,304,128]{2,1,0:T(8,128)(2,1)S(1)} all-to-all(s16[16,304,128]{2,1,0:T(8,128)(2,1)S(1)} %xc.1), channel_id=1, replica_groups=mesh['rows_0'=4,'rows_1'=2,'cols_0'=4,'cols_1'=4] {'cols_0','cols_1'}, dimensions={0} | all-to-all | bytes 2490368 | tf_op jit(solution)/shard_map/all_to_all | solution.py:35
  84.2 1.0 %merge.1 = (f32[48,768]{1,0:T(8,128)}, f32[1,48]{1,0:T(1,128)}, f32[8,128]{1,0:T(8,128)S(1)}) custom-call(s16[16,304,128]{2,1,0:T(8,128)(2,1)S(1)} %all_to_all.16.recv_ref), custom_call_target="tpu_custom_call" | custom-call | tf_op jit(solution)/shard_map/merge/pallas_call | solution.py:429
  85.2 0.0 collective-permute-start
  85.2 1.2 %collective-permute-done = f32[8,128]{1,0:T(8,128)S(1)} collective-permute-done((f32[8,128]{1,0:T(8,128)S(1)}, f32[8,128]{1,0:T(8,128)S(1)}, u32[]{:S(2)}, u32[]{:S(2)}) %collective-permute-start) | collective-permute-done | bytes 4128 | tf_op jit(solution)/shard_map/ppermute | solution.py:329
  86.4 0.3 collective-permute-start.1
  86.6 3.3 %collective-permute-done.1 = f32[8,128]{1,0:T(8,128)S(1)} collective-permute-done((f32[8,128]{1,0:T(8,128)S(1)}, f32[8,128]{1,0:T(8,128)S(1)}, u32[]{:S(2)}, u32[]{:S(2)}) %collective-permute-start.1) | collective-permute-done | bytes 4128 | tf_op jit(solution)/shard_map/ppermute | solution.py:329
  90.0 0.0 collective-permute-start.2
  90.0 4.8 %collective-permute-done.2 = f32[8,128]{1,0:T(8,128)S(1)} collective-permute-done((f32[8,128]{1,0:T(8,128)S(1)}, f32[8,128]{1,0:T(8,128)S(1)}, u32[]{:S(2)}, u32[]{:S(2)}) %collective-permute-start.2) | collective-permute-done | bytes 4128 | tf_op jit(solution)/shard_map/ppermute | solution.py:329
  94.8 0.5 slice.27
  (8 shorter events, 0.1 us)
Async XLA Ops:
  0.6 32.1 %copy-start = (f32[3,6144]{1,0:T(4,128)S(1)}, f32[3,6144]{1,0:T(4,128)}, u32[]{:S(2)}) copy-start(f32[3,6144]{1,0:T(4,128)} %param.10) | copy-start | bytes 221188
  28.1 21.7 %all-to-all-start.1 = ((bf16[16,48,768]{2,1,0:T(8,128)(2,1)}), bf16[16,48,768]{2,1,0:T(8,128)(2,1)S(1)}, u32[]{:S(2)}, u32[]{:S(2)}) async-start(bf16[16,48,768]{2,1,0:T(8,128)(2,1)} %strip.1), calls=%async_computation.1 | async-start | bytes 2359296 | tf_op jit(solution)/shard_map/all_to_all | solution.py:35
  85.2 1.2 %collective-permute-start = (f32[8,128]{1,0:T(8,128)S(1)}, f32[8,128]{1,0:T(8,128)S(1)}, u32[]{:S(2)}, u32[]{:S(2)}) collective-permute-start(f32[8,128]{1,0:T(8,128)S(1)} %get-tuple-element.14), channel_id=1, source_target_pairs={{0,16},{16,0},{1,17},{17,1},{2,18},{18,2},{3,19},{19,3},{4,20},{20... | collective-permute-start | bytes 12296 | tf_op jit(solution)/shard_map/ppermute | solution.py:329
  86.4 3.6 %collective-permute-start.1 = (f32[8,128]{1,0:T(8,128)S(1)}, f32[8,128]{1,0:T(8,128)S(1)}, u32[]{:S(2)}, u32[]{:S(2)}) collective-permute-start(f32[8,128]{1,0:T(8,128)S(1)} %add.36), channel_id=1, source_target_pairs={{0,32},{32,0},{64,96},{96,64},{1,33},{33,1},{65,97},{97,65},{2,34}... | collective-permute-start | bytes 12296 | tf_op jit(solution)/shard_map/ppermute | solution.py:329
  90.0 4.8 %collective-permute-start.2 = (f32[8,128]{1,0:T(8,128)S(1)}, f32[8,128]{1,0:T(8,128)S(1)}, u32[]{:S(2)}, u32[]{:S(2)}) collective-permute-start(f32[8,128]{1,0:T(8,128)S(1)} %add.37), channel_id=1, source_target_pairs={{0,96},{32,64},{64,32},{96,0},{1,97},{33,65},{65,33},{97,1},{2,98}... | collective-permute-start | bytes 12296 | tf_op jit(solution)/shard_map/ppermute | solution.py:329

commit v3 on v1

--- a/solution.py
+++ b/solution.py
@@ -39,7 +39,7 @@
     return 4 * lax.axis_index("cols_0") + lax.axis_index("cols_1")
 
 
-def pack_kernel(live_ref, dens_ref, pts_ref, w_ref, sig_ref, out_ref, pts_s, w_s, sig_s, tile_s, sem):
+def pack_kernel(live_ref, dens_ref, pts_ref, w_ref, sig_ref, send_ref, pts_s, w_s, sig_s, tile_s, out_ref, sem):
     strips = [
         pltpu.make_async_copy(
             dens_ref.at[d * STRIP : (d + 1) * STRIP], out_ref.at[d, :STRIP], sem.at[3 + d]
@@ -74,13 +74,21 @@
 
     tile_s[:, 8 * PER :, :] = jnp.zeros((NCOLS, 8, 128), jnp.float32)
     lax.fori_loop(0, NCOLS, one, 0)
+    for copy in strips:
+        copy.wait()
+    outs = [
+        pltpu.make_async_copy(out_ref.at[:, rows], send_ref.at[:, rows], sem.at[q])
+        for q, rows in enumerate((slice(0, STRIP), slice(STRIP, STRIP + 32)))
+    ]
+    outs[0].start()
     for d in range(NCOLS):
         rest = tile_s[d]
         for q in range(3):
             part = rest.astype(jnp.bfloat16)
             rest = rest - part.astype(jnp.float32)
             out_ref[d, STRIP:, q * 128 : (q + 1) * 128] = part
-    for copy in strips:
+    outs[1].start()
+    for copy in outs:
         copy.wait()
 
 
@@ -333,12 +341,13 @@
         pack_kernel,
         out_shape=jax.ShapeDtypeStruct((NCOLS, STRIP + 32, 384), jnp.bfloat16),
         in_specs=[SMEM, ANY, ANY, ANY, ANY],
-        out_specs=VMEM,
+        out_specs=ANY,
         scratch_shapes=[
             pltpu.VMEM((3, SLOTS, PTS), jnp.float32),
             pltpu.VMEM((SLOTS, PTS), jnp.float32),
             pltpu.VMEM((NSIG, SLOTS), jnp.int32),
             pltpu.VMEM((NCOLS, 32, 128), jnp.float32),
+            pltpu.VMEM((NCOLS, STRIP + 32, 384), jnp.bfloat16),
             pltpu.SemaphoreType.DMA((3 + NCOLS,)),
         ],
         name="pack",

time: 105 us -> 105 us (level)
  no operation moved by 1% of the time
where the time goes in v3:
time: 105 us; the launch traced here: 103 us
  Pallas kernels  32.7 us (31%)
  waiting for transfers between devices  25.1 us (24%)
  blocking collectives  23.2 us (22%)
  starting transfers between devices  19.1 us (18%)
  between operations  1.42 us (1%)
    all_to_all x1, blocking collectives, exchange(): return lax.all_to_all(blocks, COLS, split_axis=0, concat_axis=0, tiled=True)  23.2 us
    pallas_call x1, Pallas kernels, shards(): pl.pallas_call(xc_kernel, out_shape=(jax.ShapeDtypeStruct((NCOLS, SPAN *...  17.7 us
    ppermute x5, waiting for transfers between devices, over_all(): lax.ppermute(value, axis, [(a, a ^ other) for a in range(lax.axis_size(ax...  13.5 us
    pallas_call x1, Pallas kernels, shards(): pl.pallas_call(phi_kernel, out_shape=(jax.ShapeDtypeStruct((SLOTS, NSIG *...  10.5 us
    all_to_all x2, starting transfers between devices, exchange(): return lax.all_to_all(blocks, COLS, split_axis=0, concat_axis=0, tiled=True)  7.86 us
    ppermute x3, starting transfers between devices, over_all(): lax.ppermute(value, 'cols_0', [(a, (a + hop) % 4) for a in range(4)])  6.67 us
    all_to_all x2, waiting for transfers between devices, exchange(): return lax.all_to_all(blocks, COLS, split_axis=0, concat_axis=0, tiled=True)  6.06 us
    ppermute x3, waiting for transfers between devices, over_all(): lax.ppermute(value, 'cols_0', [(a, (a + hop) % 4) for a in range(4)])  5.53 us
  transfers between devices with their start and end apart: 10, of which 7 were waited for; matrix products, arithmetic and copies ran while one was open for 2% of the time, Pallas kernels for 10%

profile of v3, /device:TPU:96, one launch (start us, length us, event | category | flops | bytes accessed | tf_op | source)
XLA Modules:
  0.0 103.4 jit_solution(1541777415469822719)
XLA Ops:
  0.6 0.0 copy-start
  1.3 2.3 %pack.1 = bf16[16,80,384]{2,1,0:T(8,128)(2,1)} custom-call(s32[1]{0:T(128)S(6)} %copy.10.live_ref, bf16[768,384]{1,0:T(8,128)(2,1)} %dens_ref.1, f32[3,48,256]{2,1,0:T(8,128)} %bitcast.9, f32[48,256]{1,0:T(8,128)} %w_ref.1, s32[4,48]{1,0:T(4,128)} %bitcast.10), custom_call_target="tpu_custom_call" | custom-call | tf_op jit(solution)/shard_map/pack/pallas_call | solution.py:340
  3.7 23.2 %all_to_all.15.recv_ref = bf16[16,80,384]{2,1,0:T(8,128)(2,1)S(1)} all-to-all(bf16[16,80,384]{2,1,0:T(8,128)(2,1)} %pack.1), channel_id=1, replica_groups=mesh['rows_0'=4,'rows_1'=2,'cols_0'=4,'cols_1'=4] {'cols_0','cols_1'}, dimensions={0} | all-to-all | bytes 1966080 | tf_op jit(solution)/shard_map/all_to_all | solution.py:35
  26.9 1.2 %strip.1 = bf16[16,48,768]{2,1,0:T(8,128)(2,1)} custom-call(bf16[16,80,384]{2,1,0:T(8,128)(2,1)S(1)} %all_to_all.15.recv_ref), custom_call_target="tpu_custom_call" | custom-call | tf_op jit(solution)/shard_map/strip/pallas_call | solution.py:357
  28.1 3.8 %all-to-all-start.1 = ((bf16[16,48,768]{2,1,0:T(8,128)(2,1)}), bf16[16,48,768]{2,1,0:T(8,128)(2,1)S(1)}, u32[]{:S(2)}, u32[]{:S(2)}) async-start(bf16[16,48,768]{2,1,0:T(8,128)(2,1)} %strip.1), calls=%async_computation.1 | async-start | bytes 2359296 | tf_op jit(solution)/shard_map/all_to_all | solution.py:35
  31.9 0.8 dynamic-slice_negate_fusion
  32.7 0.0 copy-done
  32.7 0.5 broadcast_in_dim.12.basis_ref
  33.2 10.5 %phi.1 = (bf16[48,512,256]{2,1,0:T(8,128)(2,1)}, s32[64]{0:T(128)S(1)}, f32[16,32,128]{2,1,0:T(8,128)S(1)}) custom-call(s32[16,48]{1,0:T(8,128)S(1)} %bitcast.8, bf16[16,80,384]{2,1,0:T(8,128)(2,1)S(1)} %all_to_all.15.recv_ref, f32[4,768,128]{2,1,0:T(8,128)S(1)} %broadcast_in_dim.12.basis_ref), custom_call_target="tpu_custom_call" | custom-call | flops 41943040 | bytes 16777216 | tf_op jit(solution)/shard_map/phi/pallas_call | solution.py:379
  43.7 6.1 %all-to-all-done.1 = bf16[16,48,768]{2,1,0:T(8,128)(2,1)S(1)} async-done(((bf16[16,48,768]{2,1,0:T(8,128)(2,1)}), bf16[16,48,768]{2,1,0:T(8,128)(2,1)S(1)}, u32[]{:S(2)}, u32[]{:S(2)}) %all-to-all-start.1) | async-done | bytes 1179680 | tf_op jit(solution)/shard_map/all_to_all | solution.py:35
  49.7 17.7 %xc.1 = (s16[16,304,128]{2,1,0:T(8,128)(2,1)}, f32[8,128]{1,0:T(8,128)S(1)}) custom-call(s32[64]{0:T(128)S(1)} %get-tuple-element.10.list_ref, bf16[768,768]{1,0:T(8,128)(2,1)S(1)} %bitcast.7, bf16[48,512,256]{2,1,0:T(8,128)(2,1)} %get-tuple-element.11.phi_ref, f32[16,32,128]{2,1,0:T(8,128)S(1)} %get-tuple-element.12.tile_ref), custom_call_target="tpu_custom_call" | custom-call | flops 8589934592 | bytes 16777216 | tf_op jit(solution)/shard_map/xc/pallas_call | solution.py:399
  67.5 4.1 %all-to-all-start.2 = ((s16[16,304,128]{2,1,0:T(8,128)(2,1)}), s16[16,304,128]{2,1,0:T(8,128)(2,1)S(1)}, u32[]{:S(2)}, u32[]{:S(2)}) async-start(s16[16,304,128]{2,1,0:T(8,128)(2,1)} %get-tuple-element.13), calls=%async_computation.2 | async-start | bytes 2490368 | tf_op jit(solution)/shard_map/all_to_all | solution.py:35
  71.5 3.4 %collective-permute-start = (f32[8,128]{1,0:T(8,128)S(1)}, f32[8,128]{1,0:T(8,128)S(1)}, u32[]{:S(2)}, u32[]{:S(2)}) collective-permute-start(f32[8,128]{1,0:T(8,128)S(1)} %get-tuple-element.16), channel_id=1, source_target_pairs={{0,8},{4,12},{8,0},{12,4},{1,9},{5,13},{9,1},{13,5},{2,10},{6,14},... | collective-permute-start | bytes 12296 | tf_op jit(solution)/shard_map/ppermute | solution.py:327
  75.0 0.6 collective-permute-start.1
  75.5 2.7 %collective-permute-start.2 = (f32[8,128]{1,0:T(8,128)S(1)}, f32[8,128]{1,0:T(8,128)S(1)}, u32[]{:S(2)}, u32[]{:S(2)}) collective-permute-start(f32[8,128]{1,0:T(8,128)S(1)} %get-tuple-element.16), channel_id=1, source_target_pairs={{0,12},{4,0},{8,4},{12,8},{1,13},{5,1},{9,5},{13,9},{2,14},{6,2},{... | collective-permute-start | bytes 12296 | tf_op jit(solution)/shard_map/ppermute | solution.py:327
  78.2 5.5 %collective-permute-done = f32[8,128]{1,0:T(8,128)S(1)} collective-permute-done((f32[8,128]{1,0:T(8,128)S(1)}, f32[8,128]{1,0:T(8,128)S(1)}, u32[]{:S(2)}, u32[]{:S(2)}) %collective-permute-start) | collective-permute-done | bytes 4128 | tf_op jit(solution)/shard_map/ppermute | solution.py:327
  83.7 0.0 collective-permute-done.1
  83.7 0.0 collective-permute-done.2
  83.8 0.1 collective-permute-start.3
  83.8 1.2 %collective-permute-done.3 = f32[8,128]{1,0:T(8,128)S(1)} collective-permute-done((f32[8,128]{1,0:T(8,128)S(1)}, f32[8,128]{1,0:T(8,128)S(1)}, u32[]{:S(2)}, u32[]{:S(2)}) %collective-permute-start.3) | collective-permute-done | bytes 4128 | tf_op jit(solution)/shard_map/ppermute | solution.py:332
  85.0 0.3 collective-permute-start.4
  85.3 3.3 %collective-permute-done.4 = f32[8,128]{1,0:T(8,128)S(1)} collective-permute-done((f32[8,128]{1,0:T(8,128)S(1)}, f32[8,128]{1,0:T(8,128)S(1)}, u32[]{:S(2)}, u32[]{:S(2)}) %collective-permute-start.4) | collective-permute-done | bytes 4128 | tf_op jit(solution)/shard_map/ppermute | solution.py:332
  88.6 0.0 collective-permute-start.5
  88.6 4.8 %collective-permute-done.5 = f32[8,128]{1,0:T(8,128)S(1)} collective-permute-done((f32[8,128]{1,0:T(8,128)S(1)}, f32[8,128]{1,0:T(8,128)S(1)}, u32[]{:S(2)}, u32[]{:S(2)}) %collective-permute-start.5) | collective-permute-done | bytes 4128 | tf_op jit(solution)/shard_map/ppermute | solution.py:332
  93.4 1.5 %collective-permute-start.6 = (f32[8,128]{1,0:T(8,128)S(1)}, f32[8,128]{1,0:T(8,128)S(1)}, u32[]{:S(2)}, u32[]{:S(2)}) collective-permute-start(f32[8,128]{1,0:T(8,128)S(1)} %add.56), channel_id=1, source_target_pairs={{0,1},{1,0},{2,3},{3,2},{4,5},{5,4},{6,7},{7,6},{8,9},{9,8},{10,11... | collective-permute-start | bytes 12296 | tf_op jit(solution)/shard_map/ppermute | solution.py:332
  94.9 2.1 %collective-permute-done.6 = f32[8,128]{1,0:T(8,128)S(1)} collective-permute-done((f32[8,128]{1,0:T(8,128)S(1)}, f32[8,128]{1,0:T(8,128)S(1)}, u32[]{:S(2)}, u32[]{:S(2)}) %collective-permute-start.6) | collective-permute-done | bytes 4128 | tf_op jit(solution)/shard_map/ppermute | solution.py:332
  97.1 2.7 %collective-permute-start.7 = (f32[8,128]{1,0:T(8,128)S(1)}, f32[8,128]{1,0:T(8,128)S(1)}, u32[]{:S(2)}, u32[]{:S(2)}) collective-permute-start(f32[8,128]{1,0:T(8,128)S(1)} %add.57), channel_id=1, source_target_pairs={{0,3},{1,2},{2,1},{3,0},{4,7},{5,6},{6,5},{7,4},{8,11},{9,10},{10,... | collective-permute-start | bytes 12296 | tf_op jit(solution)/shard_map/ppermute | solution.py:332
  99.8 2.1 %collective-permute-done.7 = f32[8,128]{1,0:T(8,128)S(1)} collective-permute-done((f32[8,128]{1,0:T(8,128)S(1)}, f32[8,128]{1,0:T(8,128)S(1)}, u32[]{:S(2)}, u32[]{:S(2)}) %collective-permute-start.7) | collective-permute-done | bytes 4128 | tf_op jit(solution)/shard_map/ppermute | solution.py:332
  101.9 0.5 slice.27
  102.4 0.0 all-to-all-done.2.recv_ref
  102.4 1.0 merge.1
  (11 shorter events, 0.1 us)
Async XLA Ops:
  0.6 32.0 %copy-start = (f32[3,6144]{1,0:T(4,128)S(1)}, f32[3,6144]{1,0:T(4,128)}, u32[]{:S(2)}) copy-start(f32[3,6144]{1,0:T(4,128)} %param.10) | copy-start | bytes 221188
  28.1 21.7 %all-to-all-start.1 = ((bf16[16,48,768]{2,1,0:T(8,128)(2,1)}), bf16[16,48,768]{2,1,0:T(8,128)(2,1)S(1)}, u32[]{:S(2)}, u32[]{:S(2)}) async-start(bf16[16,48,768]{2,1,0:T(8,128)(2,1)} %strip.1), calls=%async_computation.1 | async-start | bytes 2359296 | tf_op jit(solution)/shard_map/all_to_all | solution.py:35
  67.5 34.9 %all-to-all-start.2 = ((s16[16,304,128]{2,1,0:T(8,128)(2,1)}), s16[16,304,128]{2,1,0:T(8,128)(2,1)S(1)}, u32[]{:S(2)}, u32[]{:S(2)}) async-start(s16[16,304,128]{2,1,0:T(8,128)(2,1)} %get-tuple-element.13), calls=%async_computation.2 | async-start | bytes 2490368 | tf_op jit(solution)/shard_map/all_to_all | solution.py:35
  71.5 12.2 %collective-permute-start = (f32[8,128]{1,0:T(8,128)S(1)}, f32[8,128]{1,0:T(8,128)S(1)}, u32[]{:S(2)}, u32[]{:S(2)}) collective-permute-start(f32[8,128]{1,0:T(8,128)S(1)} %get-tuple-element.16), channel_id=1, source_target_pairs={{0,8},{4,12},{8,0},{12,4},{1,9},{5,13},{9,1},{13,5},{2,10},{6,14},... | collective-permute-start | bytes 12296 | tf_op jit(solution)/shard_map/ppermute | solution.py:327
  75.0 8.8 %collective-permute-start.1 = (f32[8,128]{1,0:T(8,128)S(1)}, f32[8,128]{1,0:T(8,128)S(1)}, u32[]{:S(2)}, u32[]{:S(2)}) collective-permute-start(f32[8,128]{1,0:T(8,128)S(1)} %get-tuple-element.16), channel_id=1, source_target_pairs={{0,4},{4,8},{8,12},{12,0},{1,5},{5,9},{9,13},{13,1},{2,6},{6,10},{... | collective-permute-start | bytes 12296 | tf_op jit(solution)/shard_map/ppermute | solution.py:327
  75.5 8.2 %collective-permute-start.2 = (f32[8,128]{1,0:T(8,128)S(1)}, f32[8,128]{1,0:T(8,128)S(1)}, u32[]{:S(2)}, u32[]{:S(2)}) collective-permute-start(f32[8,128]{1,0:T(8,128)S(1)} %get-tuple-element.16), channel_id=1, source_target_pairs={{0,12},{4,0},{8,4},{12,8},{1,13},{5,1},{9,5},{13,9},{2,14},{6,2},{... | collective-permute-start | bytes 12296 | tf_op jit(solution)/shard_map/ppermute | solution.py:327
  83.8 1.2 %collective-permute-start.3 = (f32[8,128]{1,0:T(8,128)S(1)}, f32[8,128]{1,0:T(8,128)S(1)}, u32[]{:S(2)}, u32[]{:S(2)}) collective-permute-start(f32[8,128]{1,0:T(8,128)S(1)} %add_add_fusion), channel_id=1, source_target_pairs={{0,16},{16,0},{1,17},{17,1},{2,18},{18,2},{3,19},{19,3},{4,20},{20... | collective-permute-start | bytes 12296 | tf_op jit(solution)/shard_map/ppermute | solution.py:332
  85.0 3.6 %collective-permute-start.4 = (f32[8,128]{1,0:T(8,128)S(1)}, f32[8,128]{1,0:T(8,128)S(1)}, u32[]{:S(2)}, u32[]{:S(2)}) collective-permute-start(f32[8,128]{1,0:T(8,128)S(1)} %add.54), channel_id=1, source_target_pairs={{0,32},{32,0},{64,96},{96,64},{1,33},{33,1},{65,97},{97,65},{2,34}... | collective-permute-start | bytes 12296 | tf_op jit(solution)/shard_map/ppermute | solution.py:332
  88.6 4.8 %collective-permute-start.5 = (f32[8,128]{1,0:T(8,128)S(1)}, f32[8,128]{1,0:T(8,128)S(1)}, u32[]{:S(2)}, u32[]{:S(2)}) collective-permute-start(f32[8,128]{1,0:T(8,128)S(1)} %add.55), channel_id=1, source_target_pairs={{0,96},{32,64},{64,32},{96,0},{1,97},{33,65},{65,33},{97,1},{2,98}... | collective-permute-start | bytes 12296 | tf_op jit(solution)/shard_map/ppermute | solution.py:332
  93.4 3.6 %collective-permute-start.6 = (f32[8,128]{1,0:T(8,128)S(1)}, f32[8,128]{1,0:T(8,128)S(1)}, u32[]{:S(2)}, u32[]{:S(2)}) collective-permute-start(f32[8,128]{1,0:T(8,128)S(1)} %add.56), channel_id=1, source_target_pairs={{0,1},{1,0},{2,3},{3,2},{4,5},{5,4},{6,7},{7,6},{8,9},{9,8},{10,11... | collective-permute-start | bytes 12296 | tf_op jit(solution)/shard_map/ppermute | solution.py:332
  97.1 4.8 %collective-permute-start.7 = (f32[8,128]{1,0:T(8,128)S(1)}, f32[8,128]{1,0:T(8,128)S(1)}, u32[]{:S(2)}, u32[]{:S(2)}) collective-permute-start(f32[8,128]{1,0:T(8,128)S(1)} %add.57), channel_id=1, source_target_pairs={{0,3},{1,2},{2,1},{3,0},{4,7},{5,6},{6,5},{7,4},{8,11},{9,10},{10,... | collective-permute-start | bytes 12296 | tf_op jit(solution)/shard_map/ppermute | solution.py:332
